TPU v7x, 128 devices: a whole 4x4x4 slice. The times are simulated.
128 devices in a mesh: row: 8 (over x, core), col: 16 (over z, y).
Axes of the slice: x: 4, y: 4, z: 4, core: 2. Of those that a mesh axis runs over, the one named last changes fastest.
Arguments:
- features: float32 [32768, 128], P('col', 'row'), may hold values from -6 to 6
- tile_rows: int32 [8, 16, 80], P('row', 'col'), may hold values from 0 to 32, as said below
- tile_cols: int32 [8, 16, 80], P('row', 'col'), may hold values from 0 to 15
- tile_values: float32 [8, 16, 80, 128, 128], P('row', 'col'), may hold values from -0.51881118 to 0.51881118, as said below
- weight_in: float32 [128, 256], replicated, may hold values from -0.5 to 0.5
- weight_out: float32 [256, 256], replicated, may hold values from -0.375 to 0.375
- cotangent: float32 [32768, 256], P(('col', 'row')), may hold values from -0.03125 to 0.03125
Outputs:
- output: float32 [32768, 256], P(('col', 'row'))
- grad_in: float32 [128, 256], replicated
- grad_out: float32 [256, 256], replicated
Inputs may be any that keep to these rules, and one draw needn't show every extreme that they name: `tile_rows`: slot s of device (i, j) is used for s below that device's tile count and holds a tile row 0 to 31; unused slots hold 32. Used slots come first, no (row, column) pair repeats within a device, and in every draw some device uses all 80 slots. `tile_values`: A tile is sparse: each entry is nonzero with probability 2.56 / 128, at random positions.
All inputs are finite; a program needn't handle non-finite values.
Results may differ from a plain program's by a relative error of at most 0.0003.
Values sent between devices are 32-bit elements; how exact they have to be, the bound alone decides.
A program may use at most 128 MiB of HBM per device.

v0:
```python
import jax
import jax.numpy as jnp
from jax import lax
from jax.sharding import PartitionSpec as P

TILE = 128


def forward_tiles(gathered, tile_row, tile_col, tile_block, out_tiles):
    width = gathered.shape[1]
    blocks = gathered.reshape(-1, TILE, width)
    picked = jnp.take(blocks, tile_col, axis=0)
    products = jnp.einsum("tab,tbf->taf", tile_block, picked, precision=lax.Precision.HIGHEST)
    onehot = (tile_row[None, :] == jnp.arange(out_tiles, dtype=jnp.int32)[:, None]).astype(
        jnp.float32
    )
    summed = jnp.einsum("rt,taf->raf", onehot, products, precision=lax.Precision.HIGHEST)
    return summed.reshape(out_tiles * TILE, width)


def adjoint_tiles(row_grads, tile_row, tile_col, tile_block, out_tiles):
    width = row_grads.shape[1]
    in_tiles = row_grads.shape[0] // TILE
    blocks = row_grads.reshape(in_tiles, TILE, width)
    picked = jnp.take(blocks, jnp.minimum(tile_row, in_tiles - 1), axis=0)
    products = jnp.einsum("tba,tbf->taf", tile_block, picked, precision=lax.Precision.HIGHEST)
    matches = tile_col[None, :] == jnp.arange(out_tiles, dtype=jnp.int32)[:, None]
    onehot = (matches & (tile_row < in_tiles)[None, :]).astype(jnp.float32)
    summed = jnp.einsum("rt,taf->raf", onehot, products, precision=lax.Precision.HIGHEST)
    return summed.reshape(out_tiles * TILE, width)


def dense_product(left, right):
    return jnp.dot(left, right, precision=lax.Precision.HIGHEST, preferred_element_type=jnp.float32)


def inner_rows(left, right):
    return lax.dot_general(
        left,
        right,
        (((0,), (0,)), ((), ())),
        precision=lax.Precision.HIGHEST,
        preferred_element_type=jnp.float32,
    )


def per_device(features, tile_rows, tile_cols, tile_values, weight_in, weight_out, cotangent):
    tile_row = tile_rows.reshape(-1)
    tile_col = tile_cols.reshape(-1)
    tile_block = tile_values.reshape(-1, TILE, TILE)
    local_rows = cotangent.shape[0]
    row_tiles = lax.axis_size("col") * local_rows // TILE
    col_tiles = lax.axis_size("row") * local_rows // TILE
    x_local = lax.all_to_all(features, "row", split_axis=0, concat_axis=1, tiled=True)
    support = dense_product(x_local, weight_in)
    gathered = lax.all_gather(support, "row", axis=0, tiled=True)
    partial_one = forward_tiles(gathered, tile_row, tile_col, tile_block, row_tiles)
    pre_act = lax.psum_scatter(partial_one, "col", scatter_dimension=0, tiled=True)
    hidden = jax.nn.silu(pre_act)
    support_two = dense_product(hidden, weight_out)
    gathered_two = lax.all_gather(support_two, "row", axis=0, tiled=True)
    partial_two = forward_tiles(gathered_two, tile_row, tile_col, tile_block, row_tiles)
    output = lax.psum_scatter(partial_two, "col", scatter_dimension=0, tiled=True)
    rows_out = lax.all_gather(cotangent, "col", axis=0, tiled=True)
    adjoint_two = adjoint_tiles(rows_out, tile_row, tile_col, tile_block, col_tiles)
    d_support_two = lax.psum_scatter(adjoint_two, "row", scatter_dimension=0, tiled=True)
    grad_out_local = inner_rows(hidden, d_support_two)
    d_hidden = dense_product(d_support_two, weight_out.T)
    sigmoid_pre = jax.nn.sigmoid(pre_act)
    d_pre = d_hidden * sigmoid_pre * (1.0 + pre_act * (1.0 - sigmoid_pre))
    rows_in = lax.all_gather(d_pre, "col", axis=0, tiled=True)
    adjoint_one = adjoint_tiles(rows_in, tile_row, tile_col, tile_block, col_tiles)
    d_support = lax.psum_scatter(adjoint_one, "row", scatter_dimension=0, tiled=True)
    grad_in_local = inner_rows(x_local, d_support)
    grad_in, grad_out = lax.psum((grad_in_local, grad_out_local), ("row", "col"))
    return (output, grad_in, grad_out)


def solution(mesh):
    return jax.shard_map(
        per_device,
        mesh=mesh,
        in_specs=(
            P("col", "row"),
            P("row", "col", None),
            P("row", "col", None),
            P("row", "col", None, None, None),
            P(),
            P(),
            P(("col", "row"), None),
        ),
        out_specs=(P(("col", "row"), None), P(), P()),
        check_vma=False,
    )
```

profile of v0, /device:TPU:0, one launch (start us, length us, event | category | flops | bytes accessed | tf_op | source)
XLA Modules:
  0.0 642.4 jit_solution(13298213714380566996)
XLA Ops:
  8.9 10.3 %all_to_all.19 = f32[8,256,16]{1,2,0:T(8,128)S(1)} all-to-all(f32[8,256,16]{1,2,0:T(8,128)S(1)} %bitcast.80), channel_id=1, replica_groups=mesh['row'=8,'col'=16] {'row'}, dimensions={0} | all-to-all | bytes 262144 | tf_op jit(solution)/shard_map/all_to_all | solution.py:54
  22.0 42.2 %all-gather.9.cloned.1.call-done = f32[4096,256]{1,0:T(8,128)} async-done(((f32[256,256]{1,0:T(8,128)}), f32[4096,256]{1,0:T(8,128)}) %all-gather.9.cloned.1.call-update) | async-done | bytes 4194320 | tf_op jit(solution)/shard_map/all_gather | solution.py:64
  64.2 10.3 %gather_fusion.2 = f32[80,128,256]{2,1,0:T(8,128)} fusion(f32[32,128,256]{2,1,0:T(8,128)} %bitcast.72, s32[1024]{0:T(1024)S(1)} %pad_clamp_fusion), kind=kCustom, calls=%fused_computation.1.clone | custom fusion | bytes 20971840 | tf_op jit(solution)/shard_map/jit(_take)/gather | solution.py:25
  74.5 23.2 %fusion.30 = f32[80,128,256]{1,2,0:T(8,128)} fusion(f32[1,1,80,128,128]{4,3,2,1,0:T(8,128)} %param.14, f32[80,128,256]{2,1,0:T(8,128)} %gather_fusion.2, pred[80]{0:T(512)(128)(4,1)S(1)} %get-tuple-element.22), kind=kOutput, calls=%fused_computation.26 | convolution fusion | flops 4029153280 | bytes 26214480 | tf_op jit(solution)/shard_map/tba,tbf->taf/dot_general | solution.py:26
  97.7 11.6 %copy.48 = f32[80,128,256]{2,0,1:T(8,128)} copy(f32[80,128,256]{1,2,0:T(8,128)} %fusion.30) | data formatting | bytes 20971520 | tf_op jit(solution)/shard_map/tba,tbf->taf/dot_general | solution.py:26
  109.4 6.2 fusion.57
  118.7 9.8 %gather_fusion = f32[80,128,256]{2,1,0:T(8,128)} fusion(f32[16,128,256]{2,1,0:T(8,128)} %bitcast.70, s32[1024]{0:T(1024)S(1)} %pad_clamp_fusion.1), kind=kCustom, calls=%fused_computation.clone | custom fusion | bytes 20971840 | tf_op jit(solution)/shard_map/jit(_take)/gather | solution.py:12
  128.5 23.0 %fusion.20 = f32[80,128,256]{1,2,0:T(8,128)} fusion(f32[1,1,80,128,128]{4,3,2,1,0:T(8,128)} %param.14, f32[80,128,256]{2,1,0:T(8,128)} %gather_fusion, pred[80]{0:T(512)(128)(4,1)S(1)} %compare_and_fusion.1), kind=kOutput, calls=%fused_computation.24 | convolution fusion | flops 4029153280 | bytes 26214480 | tf_op jit(solution)/shard_map/tab,tbf->taf/dot_general | solution.py:13
  151.5 11.6 %copy.42 = f32[80,128,256]{2,0,1:T(8,128)} copy(f32[80,128,256]{1,2,0:T(8,128)} %fusion.20) | data formatting | bytes 20971520 | tf_op jit(solution)/shard_map/tab,tbf->taf/dot_general | solution.py:13
  163.1 6.9 %fusion.49 = f32[32,128,256]{2,0,1:T(8,128)S(1)} fusion(f32[80,128,256]{2,0,1:T(8,128)} %copy.42, s32[80]{0:T(128)S(1)} %bitcast.82), kind=kOutput, calls=%fused_computation.39 | convolution fusion | flops 1006635520 | bytes 14680384 | tf_op jit(solution)/shard_map/rt,taf->raf/dot_general | solution.py:17
  170.0 4.4 copy.43
  174.5 77.5 %reduce-scatter.5.cloned.1.call-done = f32[256,256]{1,0:T(8,128)} async-done(((f32[4096,256]{1,0:T(8,128)}), f32[256,256]{1,0:T(8,128)}) %reduce-scatter.5.cloned.1.call-update) | async-done | bytes 262160 | tf_op jit(solution)/shard_map/reduce_scatter | solution.py:58
  256.4 48.8 %all-gather.11.cloned.1.call-done = f32[4096,256]{1,0:T(8,128)} async-done(((f32[256,256]{1,0:T(8,128)}), f32[4096,256]{1,0:T(8,128)}) %all-gather.11.cloned.1.call-update) | async-done | bytes 4194320 | tf_op jit(solution)/shard_map/all_gather | solution.py:71
  305.2 10.5 %gather_fusion.3 = f32[80,128,256]{2,1,0:T(8,128)} fusion(f32[32,128,256]{2,1,0:T(8,128)} %bitcast.73, s32[1024]{0:T(1024)S(1)} %pad_clamp_fusion), kind=kCustom, calls=%fused_computation.3.clone | custom fusion | bytes 20971840 | tf_op jit(solution)/shard_map/jit(_take)/gather | solution.py:25
  315.8 23.2 %fusion.35 = f32[80,128,256]{1,2,0:T(8,128)} fusion(f32[1,1,80,128,128]{4,3,2,1,0:T(8,128)} %param.14, f32[80,128,256]{2,1,0:T(8,128)} %gather_fusion.3, pred[80]{0:T(512)(128)(4,1)S(1)} %get-tuple-element.22), kind=kOutput, calls=%fused_computation.27 | convolution fusion | flops 4029153280 | bytes 26214480 | tf_op jit(solution)/shard_map/tba,tbf->taf/dot_general | solution.py:26
  338.9 11.6 %copy.51 = f32[80,128,256]{2,0,1:T(8,128)} copy(f32[80,128,256]{1,2,0:T(8,128)} %fusion.35) | data formatting | bytes 20971520 | tf_op jit(solution)/shard_map/tba,tbf->taf/dot_general | solution.py:26
  350.6 6.3 fusion.55
  361.1 9.7 %gather_fusion.1 = f32[80,128,256]{2,1,0:T(8,128)} fusion(f32[16,128,256]{2,1,0:T(8,128)} %bitcast.71, s32[1024]{0:T(1024)S(1)} %pad_clamp_fusion.1), kind=kCustom, calls=%fused_computation.2.clone | custom fusion | bytes 20971840 | tf_op jit(solution)/shard_map/jit(_take)/gather | solution.py:12
  370.8 23.1 %fusion.25 = f32[80,128,256]{1,2,0:T(8,128)} fusion(f32[1,1,80,128,128]{4,3,2,1,0:T(8,128)} %param.14, f32[80,128,256]{2,1,0:T(8,128)} %gather_fusion.1, pred[80]{0:T(512)(128)(4,1)S(1)} %compare_and_fusion.1), kind=kOutput, calls=%fused_computation.25 | convolution fusion | flops 4029153280 | bytes 26214480 | tf_op jit(solution)/shard_map/tab,tbf->taf/dot_general | solution.py:13
  393.9 11.6 %copy.45 = f32[80,128,256]{2,0,1:T(8,128)} copy(f32[80,128,256]{1,2,0:T(8,128)} %fusion.25) | data formatting | bytes 20971520 | tf_op jit(solution)/shard_map/tab,tbf->taf/dot_general | solution.py:13
  408.1 6.9 %fusion.47 = f32[32,128,256]{2,0,1:T(8,128)S(1)} fusion(f32[80,128,256]{2,0,1:T(8,128)} %copy.45, s32[80]{0:T(128)S(1)} %bitcast.83), kind=kOutput, calls=%fused_computation.38 | convolution fusion | flops 1006635520 | bytes 14680384 | tf_op jit(solution)/shard_map/rt,taf->raf/dot_general | solution.py:17
  414.9 4.4 copy.46
  419.3 133.8 %all-reduce.3.cloned.1.call-done = (f32[128,256]{0,1:T(8,128)}, f32[256,256]{1,0:T(8,128)}) async-done(((f32[128,256]{0,1:T(8,128)}, f32[256,256]{1,0:T(8,128)}), (f32[128,256]{0,1:T(8,128)}, f32[256,256]{1,0:T(8,128)})) %all-reduce.3.cloned.1.call-update) | async-done | bytes 393232 | tf_op jit(solution)/shard_map/psum | solution.py:75
  554.8 79.0 %reduce-scatter.7.cloned.1.call-done = f32[256,256]{1,0:T(8,128)} async-done(((f32[4096,256]{1,0:T(8,128)}), f32[256,256]{1,0:T(8,128)}) %reduce-scatter.7.cloned.1.call-update) | async-done | bytes 262160 | tf_op jit(solution)/shard_map/reduce_scatter | solution.py:63
  (49 shorter events, 21.9 us)
Async XLA Ops:
  7.2 244.9 %copy-start = (f32[256,256]{1,0:T(8,128)S(1)}, f32[256,256]{1,0:T(8,128)}, u32[]{:S(2)}) copy-start(f32[256,256]{1,0:T(8,128)} %param.16) | copy-start | bytes 786436
  7.2 57.0 %all-gather.9.cloned.1.call-start = ((), (), s32[]{:S(2)}) async-start(), calls=%async_computation.9 | async-start | bytes 4456448 | tf_op jit(solution)/shard_map/all_gather | solution.py:64
  7.9 110.8 %all-gather.5.cloned.1.call-start = ((), (), s32[]{:S(2)}) async-start(), calls=%async_computation.5 | async-start | bytes 2359296 | tf_op jit(solution)/shard_map/all_gather | solution.py:56
  21.2 153.2 %reduce-scatter.9.cloned.1.call-start = ((), (), s32[]{:S(2)}) async-start(), calls=%async_computation.10 | async-start | bytes 2359296 | tf_op jit(solution)/shard_map/reduce_scatter | solution.py:66
  97.7 11.7 %copy-start.3 = (s32[1,1,80]{2,1,0:T(1,128)S(1)}, s32[1,1,80]{2,1,0:T(1,128)}, u32[]{:S(2)}) copy-start(s32[1,1,80]{2,1,0:T(1,128)} %param.13) | copy-start | bytes 964
  118.2 133.8 %reduce-scatter.5.cloned.1.call-start = ((), (), s32[]{:S(2)}) async-start(), calls=%async_computation.6 | async-start | bytes 4456448 | tf_op jit(solution)/shard_map/reduce_scatter | solution.py:58
  151.5 11.7 %copy-start.2 = (s32[1,1,80]{2,1,0:T(1,128)S(1)}, s32[1,1,80]{2,1,0:T(1,128)}, u32[]{:S(2)}) copy-start(s32[1,1,80]{2,1,0:T(1,128)} %param.12) | copy-start | bytes 964
  174.4 130.8 %all-gather.11.cloned.1.call-start = ((), (), s32[]{:S(2)}) async-start(), calls=%async_computation.11 | async-start | bytes 4456448 | tf_op jit(solution)/shard_map/all_gather | solution.py:71
  254.2 106.9 %all-gather.7.cloned.1.call-start = ((), (), s32[]{:S(2)}) async-start(), calls=%async_computation.7 | async-start | bytes 2359296 | tf_op jit(solution)/shard_map/all_gather | solution.py:61
  256.4 149.2 %reduce-scatter.11.cloned.1.call-start = ((), (), s32[]{:S(2)}) async-start(), calls=%async_computation.12 | async-start | bytes 2359296 | tf_op jit(solution)/shard_map/reduce_scatter | solution.py:73
  350.6 9.2 %copy-start.4 = (f32[256,256]{1,0:T(8,128)S(1)}, f32[256,256]{1,0:T(8,128)}, u32[]{:S(2)}) copy-start(f32[256,256]{1,0:T(8,128)} %reduce-scatter.9.cloned.1.call-done) | copy-start | bytes 786436
  350.6 9.2 %copy-start.5 = (f32[256,256]{1,0:T(8,128)S(1)}, f32[256,256]{1,0:T(8,128)}, u32[]{:S(2)}) copy-start(f32[256,256]{1,0:T(8,128)} %reduce-scatter.5.cloned.1.call-done) | copy-start | bytes 786436
  359.5 193.6 %all-reduce.3.cloned.1.call-start = ((), (), s32[]{:S(2)}) async-start(), calls=%async_computation.13 | async-start | bytes 786432 | tf_op jit(solution)/shard_map/psum | solution.py:75
  407.8 227.7 %copy-start.1 = (f32[256,256]{1,0:T(8,128)S(1)}, f32[256,256]{1,0:T(8,128)}, u32[]{:S(2)}) copy-start(f32[256,256]{1,0:T(8,128)} %param.16) | copy-start | bytes 786436
  407.8 226.0 %reduce-scatter.7.cloned.1.call-start = ((), (), s32[]{:S(2)}) async-start(), calls=%async_computation.8 | async-start | bytes 4456448 | tf_op jit(solution)/shard_map/reduce_scatter | solution.py:63
Sparse Core Ops, SparseCore 0:
  10.1 53.9 all-gather.8
  66.5 24.8 all-gather.4
  118.3 32.6 reduce-scatter.8
  174.5 77.4 reduce-scatter.4
  254.6 50.5 all-gather.10
  307.4 24.8 all-gather.6
  359.6 32.7 reduce-scatter.10
  407.9 145.1 all-reduce.2
  557.0 76.7 reduce-scatter.6
where the time goes:
time: 652 us; the launch traced here: 642 us
  waiting for transfers between devices  382 us (59%)
  matrix products  128 us (20%)
  local copies, waits for them, and re-layouts  105 us (16%)
  between operations  14.4 us (2%)
  blocking collectives  10.3 us (2%)
    psum x1, waiting for transfers between devices, per_device(): lax.psum((grad_in_local, grad_out_local), ('row', 'col'))  134 us
    reduce_scatter x1, waiting for transfers between devices, per_device(): lax.psum_scatter(partial_two, 'col', scatter_dimension=0, tiled=True)  79 us
    reduce_scatter x1, waiting for transfers between devices, per_device(): lax.psum_scatter(partial_one, 'col', scatter_dimension=0, tiled=True)  77.5 us
    all_gather x1, waiting for transfers between devices, per_device(): rows_in = lax.all_gather(d_pre, 'col', axis=0, tiled=True)  48.8 us
    dot_general x2, matrix products, adjoint_tiles(): jnp.einsum('tba,tbf->taf', tile_block, picked, precision=lax.Precision.HI...  46.4 us
    dot_general x2, matrix products, forward_tiles(): jnp.einsum('tab,tbf->taf', tile_block, picked, precision=lax.Precision.HI...  46.1 us
    all_gather x1, waiting for transfers between devices, per_device(): rows_out = lax.all_gather(cotangent, 'col', axis=0, tiled=True)  42.2 us
    dot_general x2, local copies, waits for them, and re-layouts, forward_tiles(): jnp.einsum('tab,tbf->taf', tile_block, picked, precision=lax.Precision.HI...  23.3 us
  transfers between devices with their start and end apart: 9, of which 5 were waited for; matrix products, arithmetic and copies ran while one was open for 36% of the time, Pallas kernels for 0%

commit v1 on v0

v1 whole, which is shorter than its diff:
```python
import functools

import jax
import jax.numpy as jnp
from jax import lax
from jax.experimental import pallas as pl
from jax.experimental.pallas import tpu as pltpu
from jax.sharding import PartitionSpec as P

MESH = pl.DeviceIdType.MESH
F32 = jnp.float32
BF16 = jnp.bfloat16
VMEM_LIMIT = 60 * 1024 * 1024
CHUNK = 8


def split(v):
    hi = v.astype(BF16)
    return hi, (v - hi.astype(F32)).astype(BF16)


def dot16(a, b, dims=(((1,), (0,)), ((), ()))):
    return lax.dot_general(a, b, dims, preferred_element_type=F32)


def dot3(a, b, dims=(((1,), (0,)), ((), ()))):
    ah, al = split(a)
    bh, bl = split(b)
    return dot16(ah, bl, dims) + dot16(al, bh, dims) + dot16(ah, bh, dims)


class Net:
    def __init__(self, send_sems, recv_sems):
        self.send_sems, self.recv_sems = send_sems, recv_sems
        self.copies = []
        i, j = lax.axis_index("row"), lax.axis_index("col")
        self.x, self.core = i // 2, lax.rem(i, 2)
        self.z, self.y = j // 4, lax.rem(j, 4)
        self.i, self.j = i, j
        self.queue = []

    def pos(self, axis):
        return {"x": self.x, "y": self.y, "z": self.z}[axis]

    def at(self, axis, shift):
        return lax.rem(self.pos(axis) + (shift + 4), 4)

    def peer(self, axis, shift):
        if axis == "core":
            return (self.x * 2 + 1 - self.core, self.j)
        p = self.at(axis, shift)
        if axis == "x":
            return (p * 2 + self.core, self.j)
        if axis == "y":
            return (self.i, self.z * 4 + p)
        return (self.i, p * 4 + self.y)

    def barrier(self, axes):
        sem = pltpu.get_barrier_semaphore()
        n = 0
        for axis in axes:
            for shift in (1,) if axis == "core" else (1, -1):
                pl.semaphore_signal(sem, inc=1, device_id=self.peer(axis, shift), device_id_type=MESH)
                n += 1
        pl.semaphore_wait(sem, n)

    def send(self, src, dst, axis, shift=1):
        k = len(self.copies)
        copy = pltpu.make_async_remote_copy(
            src_ref=src,
            dst_ref=dst,
            send_sem=self.send_sems.at[k],
            recv_sem=self.recv_sems.at[k],
            device_id=self.peer(axis, shift),
            device_id_type=MESH,
        )
        copy.start()
        self.copies.append(copy)
        return copy

    def spawn(self, gen):
        self.queue.append(gen)

    def run(self):
        while self.queue:
            gen = self.queue.pop(0)
            try:
                next(gen)
            except StopIteration:
                continue
            self.queue.append(gen)
        for copy in self.copies:
            copy.wait_send()


def ag_ring(net, axis, src, ref, have, units=2):
    p, up, down, far = net.at(axis, 0), net.at(axis, 1), net.at(axis, -1), net.at(axis, 2)
    last = units - 1
    plus, minus = {}, {}
    for u in range(units):
        plus[u] = net.send(src(u), ref(p, u), axis, 1)
        v = last - u
        minus[v] = net.send(src(v), ref(p, v), axis, -1)
    yield
    plus[0].wait_recv()
    f0 = net.send(ref(down, 0), ref(down, 0), axis, 1)
    f1 = None
    if units == 2:
        minus[1].wait_recv()
        f1 = net.send(ref(up, 1), ref(up, 1), axis, -1)
    yield
    if units == 2:
        plus[1].wait_recv()
    have(down)
    minus[0].wait_recv()
    have(up)
    yield
    f0.wait_recv()
    if f1 is not None:
        f1.wait_recv()
    have(far)


def rs_ring(net, axis, part, ready, stage, emit, units=2):
    p, up, down, far = net.at(axis, 0), net.at(axis, 1), net.at(axis, -1), net.at(axis, 2)
    r0, r1, m0, m1, q0, q1 = (stage(k) for k in range(6))
    while not ready[2]:
        yield
    a0 = net.send(part(far, 0), r0, axis, 1)
    a1 = net.send(part(far, 1), r1, axis, -1) if units == 2 else None
    while not (ready[1] and ready[-1]):
        yield
    b0 = net.send(part(down, 0), q0, axis, -1)
    b1 = net.send(part(up, 1), m1, axis, 1) if units == 2 else None
    yield
    a0.wait_recv()
    r0[...] = r0[...] + part(up, 0)[...]
    c0 = net.send(r0, m0, axis, 1)
    if units == 2:
        a1.wait_recv()
        r1[...] = r1[...] + part(down, 1)[...]
        c1 = net.send(r1, q1, axis, -1)
    while not ready[0]:
        yield
    yield
    b0.wait_recv()
    c0.wait_recv()
    emit(0, part(p, 0)[...] + (m0[...] + q0[...]))
    if units == 2:
        b1.wait_recv()
        c1.wait_recv()
        emit(1, part(p, 1)[...] + (m1[...] + q1[...]))


ALL = {0: True, 1: True, 2: True, -1: True}
SHIFTS = (2, 1, -1, 0)


def rs_plane(net, tiles, stage_one, middle, stage_two, out, done):
    for part, (first, second) in enumerate((("z", "y"), ("y", "z"))):
        ready = {d: False for d in SHIFTS}

        def block(a, b, first=first):
            return a * 4 + b if first == "z" else b * 4 + a

        for k, d in enumerate(SHIFTS):
            pos2 = net.at(second, d)
            left = [2]

            def term(pos1, u, pos2=pos2, part=part, block=block):
                return tiles.at[2 * block(pos1, pos2) + part, pl.ds(u * 64, 64), :]

            def land(s, part=part, k=k):
                return stage_one.at[part, k, s]

            def emit(u, value, part=part, pos2=pos2, d=d, left=left, ready=ready):
                middle[part, pos2, u] = value
                left[0] -= 1
                if left[0] == 0:
                    ready[d] = True

            net.spawn(rs_ring(net, first, term, ALL, land, emit))

        def term2(pos, u, part=part):
            return middle.at[part, pos, u]

        def land2(s, part=part):
            return stage_two.at[part, s]

        def emit2(u, value, part=part):
            out[pl.ds(part * 128 + u * 64, 64), :] = value
            done.append((part, u))

        net.spawn(rs_ring(net, second, term2, ready, land2, emit2))


def gather_kernel(feat_ref, cot_ref, xt_ref, cots_ref, send_sems, recv_sems, local_sems):
    net = Net(send_sems, recv_sems)
    net.barrier(("x", "core", "y", "z"))
    own = [
        pltpu.make_async_copy(feat_ref, xt_ref.at[net.i], local_sems.at[0]),
        pltpu.make_async_copy(cot_ref, cots_ref.at[net.j], local_sems.at[1]),
    ]
    for copy in own:
        copy.start()
    sibling = []

    def row_src(u):
        return feat_ref.at[pl.ds(u * 8, 8), :]

    def row_ref(pos, u):
        return xt_ref.at[pos * 2 + net.core, pl.ds(u * 8, 8), :]

    def row_have(pos):
        block = xt_ref.at[pos * 2 + net.core]
        sibling.append(net.send(block, block, "core"))

    sibling.append(net.send(feat_ref, xt_ref.at[net.i], "core"))
    net.spawn(ag_ring(net, "x", row_src, row_ref, row_have))

    for part, (first, second) in enumerate((("y", "z"), ("z", "y"))):

        def block(a, b, first=first):
            return a + b * 4 if first == "y" else a * 4 + b

        def rows(u, part=part):
            return pl.ds(part * 128 + u * 64, 64)

        def start_second(pos1, src, part=part, second=second, block=block, rows=rows):
            def ref(pos2, u):
                return cots_ref.at[block(pos1, pos2), rows(u), :]

            net.spawn(ag_ring(net, second, src, ref, lambda pos: None))

        def own_src(u, rows=rows):
            return cot_ref.at[rows(u), :]

        def ref_one(pos1, u, second=second, block=block, rows=rows):
            return cots_ref.at[block(pos1, net.at(second, 0)), rows(u), :]

        def have_one(pos1, start_second=start_second, ref_one=ref_one):
            start_second(pos1, lambda u: ref_one(pos1, u))

        net.spawn(ag_ring(net, first, own_src, ref_one, have_one))
        start_second(net.at(first, 0), own_src)
    net.run()
    for copy in sibling:
        copy.wait_recv()
    for copy in own:
        copy.wait()


def tile_copies(tiles_ref, buf, sems):
    n = tiles_ref.shape[0] // CHUNK
    return [
        pltpu.make_async_copy(tiles_ref.at[pl.ds(k * CHUNK, CHUNK)], buf.at[pl.ds(k * CHUNK, CHUNK)], sems.at[k])
        for k in range(n)
    ]


def wait_chunk(tiles_ref, buf, sems, k):
    rows = pl.ds(k * CHUNK, CHUNK)
    pltpu.make_async_copy(tiles_ref.at[rows], buf.at[rows], sems.at[k]).wait()


def first_products_kernel(rows_ref, cols_ref, tiles_ref, xt_ref, cots_ref, fwd_ref, adj_ref,
                          buf, cbuf, xh, xl, ch, cl, sems, csem):
    copies = tile_copies(tiles_ref, buf, sems)
    for copy in copies:
        copy.start()
    ccopy = pltpu.make_async_copy(cots_ref, cbuf, csem)
    ccopy.start()
    fwd_ref[...] = jnp.zeros_like(fwd_ref)
    adj_ref[...] = jnp.zeros_like(adj_ref)

    def split_x(c, _):
        h, l = split(jnp.transpose(xt_ref[:, pl.ds(pl.multiple_of(c * 128, 128), 128)]))
        xh[c] = h
        xl[c] = l
        return 0

    lax.fori_loop(0, 16, split_x, 0)

    def fwd(k, _):
        wait_chunk(tiles_ref, buf, sems, k)
        for s in range(CHUNK):
            t = k * CHUNK + s
            r, c = rows_ref[t], cols_ref[t]
            h, l = split(buf[t])
            w = jnp.concatenate([xh[c], xl[c]], axis=1)
            res = dot16(jnp.concatenate([h, l], axis=1), jnp.concatenate([w, w], axis=0))
            fwd_ref[r] += res[:, :128] + res[:, 128:]
        return 0

    lax.fori_loop(0, len(copies), fwd, 0)
    ccopy.wait()

    def split_c(r, _):
        h, l = split(cbuf[r])
        ch[r] = h
        cl[r] = l
        return 0

    lax.fori_loop(0, 32, split_c, 0)

    def adj(k, _):
        for s in range(CHUNK):
            t = k * CHUNK + s
            r, c = rows_ref[t], cols_ref[t]
            target = jnp.where(r < 32, c, 16)
            r = jnp.minimum(r, 31)
            h, l = split(jnp.transpose(buf[t]))
            w = ch[r]
            res = dot16(jnp.concatenate([h, l], axis=1), jnp.concatenate([w, w], axis=0))
            adj_ref[target] += res + dot16(h, cl[r])
        return 0

    lax.fori_loop(0, len(copies), adj, 0)


def second_product_kernel(rows_ref, cols_ref, tiles_ref, s_ref, fwd_ref, buf, xh, xl, sems):
    copies = tile_copies(tiles_ref, buf, sems)
    for copy in copies:
        copy.start()
    fwd_ref[...] = jnp.zeros_like(fwd_ref)

    def split_x(c, _):
        h, l = split(s_ref[c])
        xh[c] = h
        xl[c] = l
        return 0

    lax.fori_loop(0, 16, split_x, 0)

    def fwd(k, _):
        wait_chunk(tiles_ref, buf, sems, k)
        for s in range(CHUNK):
            t = k * CHUNK + s
            r, c = rows_ref[t], cols_ref[t]
            h, l = split(buf[t])
            w = xh[c]
            res = dot16(jnp.concatenate([h, l], axis=1), jnp.concatenate([w, w], axis=0))
            fwd_ref[r] += res + dot16(h, xl[c])
        return 0

    lax.fori_loop(0, len(copies), fwd, 0)


def middle_kernel(fwd_ref, adj_ref, win_ref, wout_ref, s2_ref, g_ref,
                  stage_a, mid_a, stage_b, s_buf, stage_c, mid_c, stage_d, d_buf, h_buf, p_buf, s2_buf,
                  g_buf, stage_e, g_one, stage_f, g_two, stage_g, send_sems, recv_sems, local_sem):
    net = Net(send_sems, recv_sems)
    net.barrier(("x", "core", "y", "z"))
    done_s, done_d, sibling = [], [], []
    rs_plane(net, fwd_ref, stage_a, mid_a, stage_b, s_buf, done_s)

    ready = {d: False for d in SHIFTS}

    def cores():
        copies = []
        for k, d in enumerate(SHIFTS):
            block = net.at("x", d) * 2 + 1 - net.core
            copies.append(net.send(adj_ref.at[pl.ds(block * 2, 2)], stage_c.at[k], "core"))
        yield
        for k, d in enumerate(SHIFTS):
            copies[k].wait_recv()
            pos = net.at("x", d)
            mid_c[pos] = adj_ref[pl.ds((pos * 2 + net.core) * 2, 2)] + stage_c[k]
            ready[d] = True
            yield

    def emit_d(u, value):
        d_buf[pl.ds(u * 128, 128), :] = value
        done_d.append(u)

    net.spawn(cores())
    net.spawn(rs_ring(net, "x", lambda pos, u: mid_c.at[pos, u], ready, lambda s: stage_d.at[s], emit_d))
    local = pltpu.make_async_copy(s2_buf, s2_ref.at[net.i], local_sem)

    def s2_have(pos):
        block = s2_ref.at[pos * 2 + net.core]
        sibling.append(net.send(block, block, "core"))

    def dense():
        while len(done_s) < 4:
            yield
        pre = dot3(s_buf[...], win_ref[...])
        hidden = pre * (1.0 / (1.0 + jnp.exp(-pre)))
        p_buf[...] = pre
        h_buf[...] = hidden
        s2_buf[...] = dot3(hidden, wout_ref[...]).reshape(2, 128, 256)
        local.start()
        sibling.append(net.send(s2_buf, s2_ref.at[net.i], "core"))
        net.spawn(ag_ring(net, "x", lambda u: s2_buf.at[u], lambda pos, u: s2_ref.at[pos * 2 + net.core, u], s2_have))
        while len(done_d) < 2:
            yield
        d = d_buf[...]
        pre = p_buf[...]
        sg = 1.0 / (1.0 + jnp.exp(-pre))
        d_pre = dot3(d, wout_ref[...], (((1,), (1,)), ((), ()))) * sg * (1.0 + pre * (1.0 - sg))
        grad_in = dot3(jnp.transpose(s_buf[...]), d_pre)
        grad_out = dot3(jnp.transpose(h_buf[...]), d)
        for c in range(2):
            lanes = slice(c * 128, c * 128 + 128)
            g_buf[c, pl.ds(0, 128), :] = grad_in[:, lanes]
            g_buf[c, pl.ds(128, 256), :] = grad_out[:, lanes]
        swap = net.send(g_buf.at[1 - net.core], stage_e, "core")
        yield
        swap.wait_recv()
        g_one[...] = (g_buf[net.core] + stage_e[...]).reshape(g_one.shape)
        one, two = [], []

        def emit_one(u, value):
            g_two[...] = value.reshape(g_two.shape)
            one.append(u)

        net.spawn(rs_ring(net, "y", lambda pos, u: g_one.at[pos], ALL, lambda s: stage_f.at[s], emit_one, units=1))
        while not one:
            yield

        def emit_two(u, value):
            g_ref[...] = value
            two.append(u)

        net.spawn(rs_ring(net, "z", lambda pos, u: g_two.at[pos], ALL, lambda s: stage_g.at[s], emit_two, units=1))

    net.spawn(dense())
    net.run()
    for copy in sibling:
        copy.wait_recv()
    local.wait()


def last_kernel(fwd_ref, g_ref, out_ref, gin_ref, gout_ref,
                stage_a, mid_a, stage_b, gx, gz, gy, gsib, send_sems, recv_sems):
    net = Net(send_sems, recv_sems)
    net.barrier(("x", "core", "y", "z"))
    done = []

    def grads():
        def walk(axis, src, dst):
            got = []
            net.spawn(ag_ring(net, axis, lambda u: src, lambda pos, u: dst.at[pos], got.append, units=1))
            while len(got) < 3:
                yield

        gx[net.x] = g_ref[...]
        yield from walk("x", g_ref, gx)
        gz[net.z] = (gx[0] + gx[1]) + (gx[2] + gx[3])
        yield from walk("z", gz.at[net.z], gz)
        gy[net.y] = gz[...].reshape(96, 128)
        yield from walk("y", gy.at[net.y], gy)
        swap = net.send(gy, gsib, "core")
        yield
        swap.wait_recv()
        mine, other = gy[...].reshape(384, 128), gsib[...].reshape(384, 128)
        first = net.core == 0
        low = jnp.where(first, mine, other)
        high = jnp.where(first, other, mine)
        gin_ref[:, :128] = low[:128]
        gin_ref[:, 128:] = high[:128]
        gout_ref[:, :128] = low[128:]
        gout_ref[:, 128:] = high[128:]

    net.spawn(grads())
    rs_plane(net, fwd_ref, stage_a, mid_a, stage_b, out_ref, done)
    net.run()


ANY = pl.BlockSpec(memory_space=pl.ANY)
VM = pl.BlockSpec(memory_space=pltpu.VMEM)
SM = pl.BlockSpec(memory_space=pltpu.SMEM)


def params(collective_id=None):
    return pltpu.CompilerParams(
        collective_id=collective_id,
        has_side_effects=collective_id is not None,
        vmem_limit_bytes=VMEM_LIMIT,
    )


def sems(n):
    return [pltpu.SemaphoreType.DMA((n,)), pltpu.SemaphoreType.DMA((n,))]


def plane_scratch(width):
    return [
        pltpu.VMEM((2, 4, 6, 64, width), F32),
        pltpu.VMEM((2, 4, 2, 64, width), F32),
        pltpu.VMEM((2, 6, 64, width), F32),
    ]


def shape(*dims):
    return jax.ShapeDtypeStruct(dims, F32)


def per_device(features, tile_rows, tile_cols, tile_values, weight_in, weight_out, cotangent):
    slots = tile_rows.shape[-1]
    rows, cols = tile_rows.reshape(slots), tile_cols.reshape(slots)
    tiles = tile_values.reshape(slots, 128, 128)

    xt, cots = pl.pallas_call(
        gather_kernel,
        out_shape=(shape(8, 16, 2048), shape(16, 256, 256)),
        in_specs=[ANY, ANY],
        out_specs=(ANY, ANY),
        scratch_shapes=sems(80) + [pltpu.SemaphoreType.DMA((2,))],
        compiler_params=params(0),
        name="gather",
    )(features.T, cotangent)

    fwd, adj = pl.pallas_call(
        first_products_kernel,
        out_shape=(shape(33, 128, 128), shape(17, 128, 256)),
        in_specs=[SM, SM, ANY, VM, ANY],
        out_specs=(VM, VM),
        scratch_shapes=[
            pltpu.VMEM((slots, 128, 128), F32),
            pltpu.VMEM((32, 128, 256), F32),
            pltpu.VMEM((16, 128, 128), BF16),
            pltpu.VMEM((16, 128, 128), BF16),
            pltpu.VMEM((32, 128, 256), BF16),
            pltpu.VMEM((32, 128, 256), BF16),
            pltpu.SemaphoreType.DMA((slots // CHUNK,)),
            pltpu.SemaphoreType.DMA,
        ],
        compiler_params=params(),
        name="first_products",
    )(rows, cols, tiles, xt.reshape(128, 2048), cots.reshape(32, 128, 256))

    s2, g = pl.pallas_call(
        middle_kernel,
        out_shape=(shape(8, 2, 128, 256), shape(24, 128)),
        in_specs=[VM, VM, VM, VM],
        out_specs=(ANY, VM),
        scratch_shapes=plane_scratch(128)
        + [
            pltpu.VMEM((256, 128), F32),
            pltpu.VMEM((4, 2, 128, 256), F32),
            pltpu.VMEM((4, 2, 128, 256), F32),
            pltpu.VMEM((6, 128, 256), F32),
            pltpu.VMEM((256, 256), F32),
            pltpu.VMEM((256, 256), F32),
            pltpu.VMEM((256, 256), F32),
            pltpu.VMEM((2, 128, 256), F32),
            pltpu.VMEM((2, 384, 128), F32),
            pltpu.VMEM((384, 128), F32),
            pltpu.VMEM((4, 96, 128), F32),
            pltpu.VMEM((6, 96, 128), F32),
            pltpu.VMEM((4, 24, 128), F32),
            pltpu.VMEM((6, 24, 128), F32),
        ]
        + sems(100)
        + [pltpu.SemaphoreType.DMA],
        compiler_params=params(1),
        name="middle",
    )(fwd, adj, weight_in, weight_out)

    fwd2 = pl.pallas_call(
        second_product_kernel,
        out_shape=shape(33, 128, 256),
        in_specs=[SM, SM, ANY, VM],
        out_specs=VM,
        scratch_shapes=[
            pltpu.VMEM((slots, 128, 128), F32),
            pltpu.VMEM((16, 128, 256), BF16),
            pltpu.VMEM((16, 128, 256), BF16),
            pltpu.SemaphoreType.DMA((slots // CHUNK,)),
        ],
        compiler_params=params(),
        name="second_product",
    )(rows, cols, tiles, s2.reshape(16, 128, 256))

    return pl.pallas_call(
        last_kernel,
        out_shape=(shape(256, 256), shape(128, 256), shape(256, 256)),
        in_specs=[VM, VM],
        out_specs=(VM, VM, VM),
        scratch_shapes=plane_scratch(256)
        + [
            pltpu.VMEM((4, 24, 128), F32),
            pltpu.VMEM((4, 24, 128), F32),
            pltpu.VMEM((4, 96, 128), F32),
            pltpu.VMEM((4, 96, 128), F32),
        ]
        + sems(80),
        compiler_params=params(2),
        name="last",
    )(fwd2, g)


def solution(mesh):
    return jax.shard_map(
        per_device,
        mesh=mesh,
        in_specs=(
            P("col", "row"),
            P("row", "col", None),
            P("row", "col", None),
            P("row", "col", None, None, None),
            P(),
            P(),
            P(("col", "row"), None),
        ),
        out_specs=(P(("col", "row"), None), P(), P()),
        check_vma=False,
    )
```

time: 652 us -> 163 us (0.25); the launches traced: 642 us -> 161 us
  waiting for transfers between devices: 382 us -> 0 us
  Pallas kernels: 0 us -> 155 us
  matrix products: 128 us -> 0 us
  local copies, waits for them, and re-layouts: 105 us -> 4.91 us
  between operations: 14.4 us -> 0.67 us
  blocking collectives: 10.3 us -> 0 us
    reduce_scatter x4 -> x0, waiting for transfers between devices: 157 us -> none  [the longest x1 79 us: per_device(): lax.psum_scatter(partial_two, 'col', scatter_dimension=0, tiled=True)]
    pallas_call x0 -> x5, Pallas kernels: none -> 155 us  [the longest x1 50.1 us: per_device(): pl.pallas_call(middle_kernel, out_shape=(shape(8, 2, 128, 256), shape(24,...]
    psum x1 -> x0, waiting for transfers between devices: 134 us -> none  [per_device(): lax.psum((grad_in_local, grad_out_local), ('row', 'col'))]
    dot_general x13 -> x0, matrix products: 128 us -> none  [the longest x2 46.4 us: adjoint_tiles(): jnp.einsum('tba,tbf->taf', tile_block, picked, precision=lax.Precision.HI...]
    all_gather x4 -> x0, waiting for transfers between devices: 91.1 us -> none  [the longest x1 48.8 us: per_device(): rows_in = lax.all_gather(d_pre, 'col', axis=0, tiled=True)]
    dot_general x8 -> x0, local copies, waits for them, and re-layouts: 60.5 us -> none  [the longest x2 23.3 us: forward_tiles(): jnp.einsum('tab,tbf->taf', tile_block, picked, precision=lax.Precision.HI...]
    gather x4 -> x0, local copies, waits for them, and re-layouts: 40.4 us -> none  [the longest x2 20.9 us: adjoint_tiles(): picked = jnp.take(blocks, jnp.minimum(tile_row, in_tiles - 1), axis=0)]
    all_to_all x1 -> x0, blocking collectives: 10.3 us -> none  [per_device(): lax.all_to_all(features, 'row', split_axis=0, concat_axis=1, tiled=True)]
  transfers between devices with their start and end apart: 9 -> 0, of which waited for: 5 -> 0; matrix products, arithmetic and copies ran while one was open for 36% -> 0% of each run, Pallas kernels for 0% -> 0%
where the time goes in v1:
time: 163 us; the launch traced here: 161 us
  Pallas kernels  155 us (95%)
  local copies, waits for them, and re-layouts  4.91 us (3%)
    pallas_call x1, Pallas kernels, per_device(): pl.pallas_call(middle_kernel, out_shape=(shape(8, 2, 128, 256), shape(24,...  50.1 us
    pallas_call x1, Pallas kernels, per_device(): pl.pallas_call(last_kernel, out_shape=(shape(256, 256), shape(128, 256),...  47.4 us
    pallas_call x1, Pallas kernels, per_device(): pl.pallas_call(gather_kernel, out_shape=(shape(8, 16, 2048), shape(16, 25...  34.4 us
    pallas_call x1, Pallas kernels, per_device(): pl.pallas_call(first_products_kernel, out_shape=(shape(33, 128, 128), sha...  13.9 us
    pallas_call x1, Pallas kernels, per_device(): pl.pallas_call(second_product_kernel, out_shape=shape(33, 128, 256), in_s...  9.13 us
    unnamed x3, local copies, waits for them, and re-layouts  4.91 us

profile of v1, /device:TPU:0, one launch (start us, length us, event | category | flops | bytes accessed | tf_op | source)
XLA Modules:
  0.0 160.5 jit_solution(5103889019531437434)
XLA Ops:
  0.6 34.4 %gather.1 = (f32[8,16,2048]{2,1,0:T(8,128)}, f32[16,256,256]{2,1,0:T(8,128)}) custom-call(f32[16,2048]{1,0:T(8,128)} %bitcast.12, f32[256,256]{1,0:T(8,128)} %cot_ref.1), custom_call_target="tpu_custom_call" | custom-call | tf_op jit(solution)/shard_map/gather/pallas_call | solution.py:504
  35.1 13.9 %first_products.1 = (f32[33,128,128]{2,1,0:T(8,128)}, f32[17,128,256]{2,1,0:T(8,128)}) custom-call(s32[80]{0:T(128)} %bitcast.13, s32[80]{0:T(128)} %bitcast.15, f32[80,128,128]{2,1,0:T(8,128)} %bitcast.7, f32[128,2048]{1,0:T(8,128)} %bitcast.11, f32[32,128,256]{2,1,0:T(8,128)} %bitcast.9), custom_call_target="tpu_custom_call" | custom-call | tf_op jit(solution)/shard_map/first_products/pallas_call | solution.py:514
  49.0 50.1 %middle.1 = (f32[8,2,128,256]{3,2,1,0:T(8,128)}, f32[24,128]{1,0:T(8,128)}) custom-call(f32[33,128,128]{2,1,0:T(8,128)} %get-tuple-element.11.fwd_ref, f32[17,128,256]{2,1,0:T(8,128)} %get-tuple-element.12.adj_ref, f32[128,256]{1,0:T(8,128)} %win_ref.1, f32[256,256]{1,0:T(8,128)} %wout_ref.1), custom_call_target="tpu_custom_call" | custom-call | tf_op jit(solution)/shard_map/middle/pallas_call | solution.py:533
  99.1 9.1 %second_product.1.fwd_ref = f32[33,128,256]{2,1,0:T(8,128)} custom-call(s32[80]{0:T(128)} %bitcast.14, s32[80]{0:T(128)} %bitcast.16, f32[80,128,128]{2,1,0:T(8,128)} %bitcast.8, f32[16,128,256]{2,1,0:T(8,128)} %bitcast.10), custom_call_target="tpu_custom_call" | custom-call | tf_op jit(solution)/shard_map/second_product/pallas_call | solution.py:561
  108.2 47.4 %last.1 = (f32[256,256]{1,0:T(8,128)}, f32[128,256]{1,0:T(8,128)}, f32[256,256]{1,0:T(8,128)}) custom-call(f32[33,128,256]{2,1,0:T(8,128)} %second_product.1.fwd_ref, f32[24,128]{1,0:T(8,128)} %get-tuple-element.14.g_ref), custom_call_target="tpu_custom_call" | custom-call | tf_op jit(solution)/shard_map/last/pallas_call | solution.py:576
  155.6 1.7 %copy.13 = f32[256,256]{1,0:T(8,128)} copy(f32[256,256]{1,0:T(8,128)} %get-tuple-element.18) | data formatting | bytes 524288
  157.3 1.6 copy.14
  158.9 1.7 %copy.15 = f32[256,256]{1,0:T(8,128)} copy(f32[256,256]{1,0:T(8,128)} %get-tuple-element.20) | data formatting | bytes 524288

commit v2 on v1

v2 whole, which is shorter than its diff:
```python
import heapq
import math

import jax
import jax.numpy as jnp
from jax import lax
from jax.experimental import pallas as pl
from jax.experimental.pallas import tpu as pltpu
from jax.sharding import PartitionSpec as P

MESH = pl.DeviceIdType.MESH
F32 = jnp.float32
BF16 = jnp.bfloat16
VMEM_LIMIT = 60 * 1024 * 1024
CHUNK = 8


def split(v):
    hi = v.astype(BF16)
    return hi, (v - hi.astype(F32)).astype(BF16)


def dot16(a, b, dims=(((1,), (0,)), ((), ()))):
    return lax.dot_general(a, b, dims, preferred_element_type=F32)


def dot3(a, b, dims=(((1,), (0,)), ((), ()))):
    ah, al = split(a)
    bh, bl = split(b)
    return dot16(ah, bl, dims) + dot16(al, bh, dims) + dot16(ah, bh, dims)


class Copy:
    def __init__(self, src, dst, axis, shift):
        self.src, self.dst, self.axis, self.shift = src, dst, axis, shift
        self.bytes = 4 * math.prod(src.shape)
        self.copy = self.arrival = None


RATE = {"x": 45e3, "y": 45e3, "z": 45e3, "core": 250e3}
DELAY = {"x": 1.6, "y": 1.6, "z": 1.6, "core": 1.0}
WINDOW = 2.5


class Net:
    def __init__(self, send_sems, recv_sems):
        self.send_sems, self.recv_sems = send_sems, recv_sems
        self.copies = []
        i, j = lax.axis_index("row"), lax.axis_index("col")
        self.x, self.core = i // 2, lax.rem(i, 2)
        self.z, self.y = j // 4, lax.rem(j, 4)
        self.i, self.j = i, j
        self.active, self.pending, self.free = [], {}, {}
        self.now, self.count = 0.0, 0

    def pos(self, axis):
        return {"x": self.x, "y": self.y, "z": self.z}[axis]

    def at(self, axis, shift):
        return lax.rem(self.pos(axis) + (shift + 4), 4)

    def peer(self, axis, shift):
        if axis == "core":
            return (self.x * 2 + 1 - self.core, self.j)
        p = self.at(axis, shift)
        if axis == "x":
            return (p * 2 + self.core, self.j)
        if axis == "y":
            return (self.i, self.z * 4 + p)
        return (self.i, p * 4 + self.y)

    def barrier(self, axes):
        sem = pltpu.get_barrier_semaphore()
        n = 0
        for axis in axes:
            for shift in (1,) if axis == "core" else (1, -1):
                pl.semaphore_signal(sem, inc=1, device_id=self.peer(axis, shift), device_id_type=MESH)
                n += 1
        pl.semaphore_wait(sem, n)

    def send(self, src, dst, axis, shift=1, level=5):
        copy = Copy(src, dst, axis, shift)
        self.count += 1
        heapq.heappush(self.pending.setdefault((axis, shift), []), (level, self.count, copy))
        return copy

    def pump(self):
        for link, heap in self.pending.items():
            while heap and self.free.get(link, 0.0) < self.now + WINDOW:
                one = heapq.heappop(heap)[2]
                k = len(self.copies)
                one.copy = pltpu.make_async_remote_copy(
                    src_ref=one.src,
                    dst_ref=one.dst,
                    send_sem=self.send_sems.at[k],
                    recv_sem=self.recv_sems.at[k],
                    device_id=self.peer(one.axis, one.shift),
                    device_id_type=MESH,
                )
                one.copy.start()
                self.copies.append(one.copy)
                end = max(self.now, self.free.get(link, 0.0)) + one.bytes / RATE[one.axis]
                self.free[link] = end
                one.arrival = end + DELAY[one.axis]

    def spawn(self, gen):
        self.active.append([gen, None])

    def run(self):
        while True:
            moved = True
            while moved:
                moved = False
                for entry in list(self.active):
                    if entry[1] is None or (callable(entry[1]) and entry[1]()):
                        moved = True
                        self.step(entry)
            self.pump()
            waits = [e for e in self.active if isinstance(e[1], Copy) and e[1].arrival is not None]
            if waits:
                entry = min(waits, key=lambda e: e[1].arrival)
                self.now = max(self.now, entry[1].arrival)
                entry[1].copy.wait_recv()
                self.step(entry)
            elif any(self.pending.values()):
                self.now = min(self.free.get(link, 0.0) for link, heap in self.pending.items() if heap)
            else:
                break
        assert not self.active
        for copy in self.copies:
            copy.wait_send()

    def step(self, entry):
        try:
            entry[1] = next(entry[0])
        except StopIteration:
            self.active.remove(entry)


def arrive(copy, have=None):
    yield copy
    if have is not None:
        have()


def ag_unit(net, axis, src, ref, have, way, level=5):
    p = net.at(axis, 0)
    near = net.send(src, ref(p), axis, way, level)
    other = net.send(src, ref(p), axis, -way, level)

    def chain():
        yield near
        pos = net.at(axis, -way)
        onward = net.send(ref(pos), ref(pos), axis, way, level)
        have(pos)
        yield onward
        have(net.at(axis, 2))

    net.spawn(chain())
    net.spawn(arrive(other, lambda: have(net.at(axis, way))))


def rs_unit(net, axis, part, ready, stage, emit, way, level=5, after=None):
    r, m, q = (stage(k) for k in range(3))
    box = []
    after = level if after is None else after

    def near():
        yield lambda: ready[-way]
        box.append(net.send(part(net.at(axis, -way)), q, axis, -way, level))

    def far():
        yield lambda: ready[2]
        first = net.send(part(net.at(axis, 2)), r, axis, way, level)
        yield first
        yield lambda: ready[way]
        r[...] = r[...] + part(net.at(axis, way))[...]
        yield net.send(r, m, axis, way, after)
        yield lambda: box
        yield box[0]
        yield lambda: ready[0]
        emit(part(net.at(axis, 0))[...] + (m[...] + q[...]))

    net.spawn(far())
    net.spawn(near())


ALL = {0: True, 1: True, 2: True, -1: True}
SHIFTS = (2, 1, -1, 0)
WAYS = (1, -1)


def rs_plane(net, tiles, stage_one, middle, stage_two, out, done):
    for part, (first, second) in enumerate((("z", "y"), ("y", "z"))):
        for u, way in enumerate(WAYS):
            ready = {d: False for d in SHIFTS}
            for k, d in enumerate((2, way, -way, 0)):
                pos2 = net.at(second, d)

                def term(pos1, pos2=pos2, part=part, u=u, first=first):
                    block = pos1 * 4 + pos2 if first == "z" else pos2 * 4 + pos1
                    return tiles.at[2 * block + part, pl.ds(u * 64, 64), :]

                def land(s, part=part, u=u, k=k):
                    return stage_one.at[part, k, u, s]

                def emit(value, part=part, u=u, pos2=pos2, d=d, ready=ready):
                    middle[part, pos2, u] = value
                    ready[d] = True

                rs_unit(net, first, term, ALL, land, emit, way, level=3 + k, after=2)

            def term2(pos, part=part, u=u):
                return middle.at[part, pos, u]

            def land2(s, part=part, u=u):
                return stage_two.at[part, u, s]

            def emit2(value, part=part, u=u):
                out[pl.ds(part * 128 + u * 64, 64), :] = value
                done.append((part, u))

            rs_unit(net, second, term2, ready, land2, emit2, way, level=1)


def gather_kernel(feat_ref, cot_ref, xt_ref, cots_ref, send_sems, recv_sems, local_sems):
    net = Net(send_sems, recv_sems)
    net.barrier(("x", "core", "y", "z"))
    own = [
        pltpu.make_async_copy(feat_ref, xt_ref.at[net.i], local_sems.at[0]),
        pltpu.make_async_copy(cot_ref, cots_ref.at[net.j], local_sems.at[1]),
    ]
    for copy in own:
        copy.start()

    def to_sibling(src, dst):
        net.spawn(arrive(net.send(src, dst, "core")))

    for u, way in enumerate(WAYS):
        half = pl.ds(u * 8, 8)

        def row_ref(pos, half=half):
            return xt_ref.at[pos * 2 + net.core, half, :]

        def row_have(pos, row_ref=row_ref):
            to_sibling(row_ref(pos), row_ref(pos))

        ag_unit(net, "x", feat_ref.at[half, :], row_ref, row_have, way)
    to_sibling(feat_ref, xt_ref.at[net.i])

    for part, (first, second) in enumerate((("y", "z"), ("z", "y"))):
        for u, way in enumerate(WAYS):
            rows = pl.ds(part * 128 + u * 64, 64)

            def ref(pos1, pos2, rows=rows, first=first):
                block = pos1 + pos2 * 4 if first == "y" else pos1 * 4 + pos2
                return cots_ref.at[block, rows, :]

            def start_second(pos1, src=None, ref=ref, second=second, way=way):
                src = ref(pos1, net.at(second, 0)) if src is None else src
                ag_unit(net, second, src, lambda pos2: ref(pos1, pos2), lambda pos: None, way)

            ag_unit(net, first, cot_ref.at[rows, :], lambda pos1, ref=ref, second=second: ref(pos1, net.at(second, 0)),
                    start_second, way, level=1)
            start_second(net.at(first, 0), cot_ref.at[rows, :])
    net.run()
    for copy in own:
        copy.wait()


def tile_copies(tiles_ref, buf, sems):
    n = tiles_ref.shape[0] // CHUNK
    return [
        pltpu.make_async_copy(tiles_ref.at[pl.ds(k * CHUNK, CHUNK)], buf.at[pl.ds(k * CHUNK, CHUNK)], sems.at[k])
        for k in range(n)
    ]


def wait_chunk(tiles_ref, buf, sems, k):
    rows = pl.ds(k * CHUNK, CHUNK)
    pltpu.make_async_copy(tiles_ref.at[rows], buf.at[rows], sems.at[k]).wait()


def first_products_kernel(rows_ref, cols_ref, tiles_ref, xt_ref, cots_ref, fwd_ref, adj_ref,
                          buf, cbuf, xh, xl, ch, cl, sems, csem):
    copies = tile_copies(tiles_ref, buf, sems)
    for copy in copies:
        copy.start()
    ccopy = pltpu.make_async_copy(cots_ref, cbuf, csem)
    ccopy.start()
    fwd_ref[...] = jnp.zeros_like(fwd_ref)
    adj_ref[...] = jnp.zeros_like(adj_ref)

    def split_x(c, _):
        h, l = split(jnp.transpose(xt_ref[:, pl.ds(pl.multiple_of(c * 128, 128), 128)]))
        xh[c] = h
        xl[c] = l
        return 0

    lax.fori_loop(0, 16, split_x, 0)

    def fwd(k, _):
        wait_chunk(tiles_ref, buf, sems, k)
        for s in range(CHUNK):
            t = k * CHUNK + s
            r, c = rows_ref[t], cols_ref[t]
            h, l = split(buf[t])
            w = jnp.concatenate([xh[c], xl[c]], axis=1)
            res = dot16(jnp.concatenate([h, l], axis=1), jnp.concatenate([w, w], axis=0))
            fwd_ref[r] += res[:, :128] + res[:, 128:]
        return 0

    lax.fori_loop(0, len(copies), fwd, 0)
    ccopy.wait()

    def split_c(r, _):
        h, l = split(cbuf[r])
        ch[r] = h
        cl[r] = l
        return 0

    lax.fori_loop(0, 32, split_c, 0)

    def adj(k, _):
        for s in range(CHUNK):
            t = k * CHUNK + s
            r, c = rows_ref[t], cols_ref[t]
            target = jnp.where(r < 32, c, 16)
            r = jnp.minimum(r, 31)
            h, l = split(jnp.transpose(buf[t]))
            w = ch[r]
            res = dot16(jnp.concatenate([h, l], axis=1), jnp.concatenate([w, w], axis=0))
            adj_ref[target] += res + dot16(h, cl[r])
        return 0

    lax.fori_loop(0, len(copies), adj, 0)


def second_product_kernel(rows_ref, cols_ref, tiles_ref, s_ref, fwd_ref, buf, xh, xl, sems):
    copies = tile_copies(tiles_ref, buf, sems)
    for copy in copies:
        copy.start()
    fwd_ref[...] = jnp.zeros_like(fwd_ref)

    def split_x(c, _):
        h, l = split(s_ref[c])
        xh[c] = h
        xl[c] = l
        return 0

    lax.fori_loop(0, 16, split_x, 0)

    def fwd(k, _):
        wait_chunk(tiles_ref, buf, sems, k)
        for s in range(CHUNK):
            t = k * CHUNK + s
            r, c = rows_ref[t], cols_ref[t]
            h, l = split(buf[t])
            w = xh[c]
            res = dot16(jnp.concatenate([h, l], axis=1), jnp.concatenate([w, w], axis=0))
            fwd_ref[r] += res + dot16(h, xl[c])
        return 0

    lax.fori_loop(0, len(copies), fwd, 0)


def middle_kernel(fwd_ref, adj_ref, win_ref, wout_ref, s2_ref, g_ref,
                  stage_a, mid_a, stage_b, s_buf, stage_c, mid_c, stage_d, d_buf, h_buf, p_buf, s2_buf,
                  g_buf, stage_e, g_one, stage_f, g_two, stage_g, send_sems, recv_sems, local_sem):
    net = Net(send_sems, recv_sems)
    net.barrier(("x", "core", "y", "z"))
    done_s, done_d = [], []
    rs_plane(net, fwd_ref, stage_a, mid_a, stage_b, s_buf, done_s)

    for u, way in enumerate(WAYS):
        ready = {d: False for d in SHIFTS}
        for k, d in enumerate((2, way, -way, 0)):
            pos = net.at("x", d)

            def cores(u=u, k=k, d=d, pos=pos, ready=ready):
                block = pos * 2 + 1 - net.core
                land = stage_c.at[u, k]
                yield net.send(adj_ref.at[block * 2 + u], land, "core", 1, k)
                mid_c[u, pos] = adj_ref[(pos * 2 + net.core) * 2 + u] + land[...]
                ready[d] = True

            net.spawn(cores())

        def emit_d(value, u=u):
            d_buf[pl.ds(u * 128, 128), :] = value
            done_d.append(u)

        rs_unit(net, "x", lambda pos, u=u: mid_c.at[u, pos], ready, lambda s, u=u: stage_d.at[u, s], emit_d, way)
    local = pltpu.make_async_copy(s2_buf, s2_ref.at[net.i], local_sem)

    def dense():
        yield lambda: len(done_s) == 4
        pre = dot3(s_buf[...], win_ref[...])
        hidden = pre * (1.0 / (1.0 + jnp.exp(-pre)))
        p_buf[...] = pre
        h_buf[...] = hidden
        s2_buf[...] = dot3(hidden, wout_ref[...]).reshape(2, 128, 256)
        local.start()
        net.now += 1.5
        for u, way in enumerate(WAYS):

            def ref(pos, u=u):
                return s2_ref.at[pos * 2 + net.core, u]

            def have(pos, ref=ref):
                net.spawn(arrive(net.send(ref(pos), ref(pos), "core")))

            ag_unit(net, "x", s2_buf.at[u], ref, have, way)
        net.spawn(arrive(net.send(s2_buf, s2_ref.at[net.i], "core")))
        net.spawn(grads())

    def grads():
        yield lambda: len(done_d) == 2
        net.pump()
        d = d_buf[...]
        pre = p_buf[...]
        sg = 1.0 / (1.0 + jnp.exp(-pre))
        d_pre = dot3(d, wout_ref[...], (((1,), (1,)), ((), ()))) * sg * (1.0 + pre * (1.0 - sg))
        grad_in = dot3(jnp.transpose(s_buf[...]), d_pre)
        grad_out = dot3(jnp.transpose(h_buf[...]), d)
        for c in range(2):
            lanes = slice(c * 128, c * 128 + 128)
            g_buf[c, pl.ds(0, 128), :] = grad_in[:, lanes]
            g_buf[c, pl.ds(128, 256), :] = grad_out[:, lanes]
        net.now += 2.0
        yield net.send(g_buf.at[1 - net.core], stage_e, "core", 1, 0)
        g_one[...] = (g_buf[net.core] + stage_e[...]).reshape(g_one.shape)
        one = []

        def emit_one(value):
            g_two[...] = value.reshape(g_two.shape)
            one.append(0)

        rs_unit(net, "y", lambda pos: g_one.at[pos], ALL, lambda s: stage_f.at[s], emit_one, 1)
        yield lambda: one

        def emit_two(value):
            g_ref[...] = value

        rs_unit(net, "z", lambda pos: g_two.at[pos], ALL, lambda s: stage_g.at[s], emit_two, 1)

    net.spawn(dense())
    net.run()
    local.wait()


def last_kernel(fwd_ref, g_ref, out_ref, gin_ref, gout_ref,
                stage_a, mid_a, stage_b, gx, gz, gy, gsib, send_sems, recv_sems):
    net = Net(send_sems, recv_sems)
    net.barrier(("x", "core", "y", "z"))

    def grads():
        def walk(axis, src, dst):
            got = []
            ag_unit(net, axis, src, lambda pos: dst.at[pos], got.append, 1, 0)
            yield lambda: len(got) == 3

        gx[net.x] = g_ref[...]
        yield from walk("x", g_ref, gx)
        gz[net.z] = (gx[0] + gx[1]) + (gx[2] + gx[3])
        yield from walk("z", gz.at[net.z], gz)
        gy[net.y] = gz[...].reshape(96, 128)
        yield from walk("y", gy.at[net.y], gy)
        yield net.send(gy, gsib, "core", 1, 0)
        mine, other = gy[...].reshape(384, 128), gsib[...].reshape(384, 128)
        first = net.core == 0
        low = jnp.where(first, mine, other)
        high = jnp.where(first, other, mine)
        gin_ref[:, :128] = low[:128]
        gin_ref[:, 128:] = high[:128]
        gout_ref[:, :128] = low[128:]
        gout_ref[:, 128:] = high[128:]

    net.spawn(grads())
    rs_plane(net, fwd_ref, stage_a, mid_a, stage_b, out_ref, [])
    net.run()


ANY = pl.BlockSpec(memory_space=pl.ANY)
VM = pl.BlockSpec(memory_space=pltpu.VMEM)
SM = pl.BlockSpec(memory_space=pltpu.SMEM)


def params(collective_id=None):
    return pltpu.CompilerParams(
        collective_id=collective_id,
        has_side_effects=collective_id is not None,
        vmem_limit_bytes=VMEM_LIMIT,
    )


def sems(n):
    return [pltpu.SemaphoreType.DMA((n,)), pltpu.SemaphoreType.DMA((n,))]


def plane_scratch(width):
    return [
        pltpu.VMEM((2, 4, 2, 3, 64, width), F32),
        pltpu.VMEM((2, 4, 2, 64, width), F32),
        pltpu.VMEM((2, 2, 3, 64, width), F32),
    ]


def shape(*dims):
    return jax.ShapeDtypeStruct(dims, F32)


def per_device(features, tile_rows, tile_cols, tile_values, weight_in, weight_out, cotangent):
    slots = tile_rows.shape[-1]
    rows, cols = tile_rows.reshape(slots), tile_cols.reshape(slots)
    tiles = tile_values.reshape(slots, 128, 128)

    xt, cots = pl.pallas_call(
        gather_kernel,
        out_shape=(shape(8, 16, 2048), shape(16, 256, 256)),
        in_specs=[ANY, ANY],
        out_specs=(ANY, ANY),
        scratch_shapes=sems(100) + [pltpu.SemaphoreType.DMA((2,))],
        compiler_params=params(0),
        name="gather",
    )(features.T, cotangent)

    fwd, adj = pl.pallas_call(
        first_products_kernel,
        out_shape=(shape(33, 128, 128), shape(17, 128, 256)),
        in_specs=[SM, SM, ANY, VM, ANY],
        out_specs=(VM, VM),
        scratch_shapes=[
            pltpu.VMEM((slots, 128, 128), F32),
            pltpu.VMEM((32, 128, 256), F32),
            pltpu.VMEM((16, 128, 128), BF16),
            pltpu.VMEM((16, 128, 128), BF16),
            pltpu.VMEM((32, 128, 256), BF16),
            pltpu.VMEM((32, 128, 256), BF16),
            pltpu.SemaphoreType.DMA((slots // CHUNK,)),
            pltpu.SemaphoreType.DMA,
        ],
        compiler_params=params(),
        name="first_products",
    )(rows, cols, tiles, xt.reshape(128, 2048), cots.reshape(32, 128, 256))

    s2, g = pl.pallas_call(
        middle_kernel,
        out_shape=(shape(8, 2, 128, 256), shape(24, 128)),
        in_specs=[VM, VM, VM, VM],
        out_specs=(ANY, VM),
        scratch_shapes=plane_scratch(128)
        + [
            pltpu.VMEM((256, 128), F32),
            pltpu.VMEM((2, 4, 128, 256), F32),
            pltpu.VMEM((2, 4, 128, 256), F32),
            pltpu.VMEM((2, 3, 128, 256), F32),
            pltpu.VMEM((256, 256), F32),
            pltpu.VMEM((256, 256), F32),
            pltpu.VMEM((256, 256), F32),
            pltpu.VMEM((2, 128, 256), F32),
            pltpu.VMEM((2, 384, 128), F32),
            pltpu.VMEM((384, 128), F32),
            pltpu.VMEM((4, 96, 128), F32),
            pltpu.VMEM((3, 96, 128), F32),
            pltpu.VMEM((4, 24, 128), F32),
            pltpu.VMEM((3, 24, 128), F32),
        ]
        + sems(120)
        + [pltpu.SemaphoreType.DMA],
        compiler_params=params(1),
        name="middle",
    )(fwd, adj, weight_in, weight_out)

    fwd2 = pl.pallas_call(
        second_product_kernel,
        out_shape=shape(33, 128, 256),
        in_specs=[SM, SM, ANY, VM],
        out_specs=VM,
        scratch_shapes=[
            pltpu.VMEM((slots, 128, 128), F32),
            pltpu.VMEM((16, 128, 256), BF16),
            pltpu.VMEM((16, 128, 256), BF16),
            pltpu.SemaphoreType.DMA((slots // CHUNK,)),
        ],
        compiler_params=params(),
        name="second_product",
    )(rows, cols, tiles, s2.reshape(16, 128, 256))

    return pl.pallas_call(
        last_kernel,
        out_shape=(shape(256, 256), shape(128, 256), shape(256, 256)),
        in_specs=[VM, VM],
        out_specs=(VM, VM, VM),
        scratch_shapes=plane_scratch(256)
        + [
            pltpu.VMEM((4, 24, 128), F32),
            pltpu.VMEM((4, 24, 128), F32),
            pltpu.VMEM((4, 96, 128), F32),
            pltpu.VMEM((4, 96, 128), F32),
        ]
        + sems(100),
        compiler_params=params(2),
        name="last",
    )(fwd2, g)


def solution(mesh):
    return jax.shard_map(
        per_device,
        mesh=mesh,
        in_specs=(
            P("col", "row"),
            P("row", "col", None),
            P("row", "col", None),
            P("row", "col", None, None, None),
            P(),
            P(),
            P(("col", "row"), None),
        ),
        out_specs=(P(("col", "row"), None), P(), P()),
        check_vma=False,
    )
```

time: 163 us -> 134 us (0.82)
  Pallas kernels: 155 us -> 127 us
    pallas_call x1, Pallas kernels: 47.4 us -> 33 us  [per_device(): pl.pallas_call(last_kernel, out_shape=(shape(256, 256), shape(128, 256),...]
    pallas_call x1, Pallas kernels: 50.1 us -> 37.7 us  [per_device(): pl.pallas_call(middle_kernel, out_shape=(shape(8, 2, 128, 256), shape(24,...]
where the time goes in v2:
time: 134 us; the launch traced here: 133 us
  Pallas kernels  127 us (95%)
  local copies, waits for them, and re-layouts  4.91 us (4%)
    pallas_call x1, Pallas kernels, per_device(): pl.pallas_call(middle_kernel, out_shape=(shape(8, 2, 128, 256), shape(24,...  37.7 us
    pallas_call x1, Pallas kernels, per_device(): pl.pallas_call(gather_kernel, out_shape=(shape(8, 16, 2048), shape(16, 25...  33.6 us
    pallas_call x1, Pallas kernels, per_device(): pl.pallas_call(last_kernel, out_shape=(shape(256, 256), shape(128, 256),...  33 us
    pallas_call x1, Pallas kernels, per_device(): pl.pallas_call(first_products_kernel, out_shape=(shape(33, 128, 128), sha...  13.8 us
    pallas_call x1, Pallas kernels, per_device(): pl.pallas_call(second_product_kernel, out_shape=shape(33, 128, 256), in_s...  9.13 us
    unnamed x3, local copies, waits for them, and re-layouts  4.91 us

profile of v2, /device:TPU:0, one launch (start us, length us, event | category | flops | bytes accessed | tf_op | source)
XLA Modules:
  0.0 132.9 jit_solution(11122287556677287604)
XLA Ops:
  0.6 33.6 %gather.1 = (f32[8,16,2048]{2,1,0:T(8,128)}, f32[16,256,256]{2,1,0:T(8,128)}) custom-call(f32[16,2048]{1,0:T(8,128)} %bitcast.12, f32[256,256]{1,0:T(8,128)} %cot_ref.1), custom_call_target="tpu_custom_call" | custom-call | tf_op jit(solution)/shard_map/gather/pallas_call | solution.py:518
  34.2 13.8 %first_products.1 = (f32[33,128,128]{2,1,0:T(8,128)}, f32[17,128,256]{2,1,0:T(8,128)}) custom-call(s32[80]{0:T(128)} %bitcast.13, s32[80]{0:T(128)} %bitcast.15, f32[80,128,128]{2,1,0:T(8,128)} %bitcast.7, f32[128,2048]{1,0:T(8,128)} %bitcast.11, f32[32,128,256]{2,1,0:T(8,128)} %bitcast.9), custom_call_target="tpu_custom_call" | custom-call | tf_op jit(solution)/shard_map/first_products/pallas_call | solution.py:528
  48.1 37.7 %middle.1 = (f32[8,2,128,256]{3,2,1,0:T(8,128)}, f32[24,128]{1,0:T(8,128)}) custom-call(f32[33,128,128]{2,1,0:T(8,128)} %get-tuple-element.11.fwd_ref, f32[17,128,256]{2,1,0:T(8,128)} %get-tuple-element.12.adj_ref, f32[128,256]{1,0:T(8,128)} %win_ref.1, f32[256,256]{1,0:T(8,128)} %wout_ref.1), custom_call_target="tpu_custom_call" | custom-call | tf_op jit(solution)/shard_map/middle/pallas_call | solution.py:547
  85.8 9.1 %second_product.1.fwd_ref = f32[33,128,256]{2,1,0:T(8,128)} custom-call(s32[80]{0:T(128)} %bitcast.14, s32[80]{0:T(128)} %bitcast.16, f32[80,128,128]{2,1,0:T(8,128)} %bitcast.8, f32[16,128,256]{2,1,0:T(8,128)} %bitcast.10), custom_call_target="tpu_custom_call" | custom-call | tf_op jit(solution)/shard_map/second_product/pallas_call | solution.py:575
  94.9 33.0 %last.1 = (f32[256,256]{1,0:T(8,128)}, f32[128,256]{1,0:T(8,128)}, f32[256,256]{1,0:T(8,128)}) custom-call(f32[33,128,256]{2,1,0:T(8,128)} %second_product.1.fwd_ref, f32[24,128]{1,0:T(8,128)} %get-tuple-element.14.g_ref), custom_call_target="tpu_custom_call" | custom-call | tf_op jit(solution)/shard_map/last/pallas_call | solution.py:590
  128.0 1.7 %copy.13 = f32[256,256]{1,0:T(8,128)} copy(f32[256,256]{1,0:T(8,128)} %get-tuple-element.18) | data formatting | bytes 524288
  129.6 1.6 %copy.14 = f32[128,256]{1,0:T(8,128)} copy(f32[128,256]{1,0:T(8,128)} %get-tuple-element.19) | data formatting | bytes 262144
  131.2 1.7 %copy.15 = f32[256,256]{1,0:T(8,128)} copy(f32[256,256]{1,0:T(8,128)} %get-tuple-element.20) | data formatting | bytes 524288

commit v3 on v0

v3 whole, which is shorter than its diff:
```python
import heapq
import math
import types

import jax
import jax.numpy as jnp
from jax import lax
from jax.experimental import pallas as pl
from jax.experimental.pallas import tpu as pltpu
from jax.sharding import PartitionSpec as P

MESH = pl.DeviceIdType.MESH
F32 = jnp.float32
BF16 = jnp.bfloat16
VMEM_LIMIT = 67043328
CHUNK = 8
SLOTS = 80
TROWS = 32
TCOLS = 16
COPIES = 240


def split(v):
    hi = v.astype(BF16)
    return hi, (v - hi.astype(F32)).astype(BF16)


def dot16(a, b, dims=(((1,), (0,)), ((), ()))):
    return lax.dot_general(a, b, dims, preferred_element_type=F32)


def dot3(a, b, dims=(((1,), (0,)), ((), ()))):
    ah, al = split(a)
    bh, bl = split(b)
    return dot16(ah, bl, dims) + dot16(al, bh, dims) + dot16(ah, bh, dims)


class Copy:
    def __init__(self, src, dst, axis, shift):
        self.src, self.dst, self.axis, self.shift = src, dst, axis, shift
        self.bytes = 4 * math.prod(src.shape)
        self.copy = self.arrival = None


RATE = {"x": 45e3, "y": 45e3, "z": 45e3, "core": 250e3}
DELAY = {"x": 1.6, "y": 1.6, "z": 1.6, "core": 1.0}
WINDOW = 2.5


class Tick:
    def __init__(self, net, spent, level):
        net.now += spent
        self.arrival = net.now + level * 1e-3


class Net:
    def __init__(self, send_sems, recv_sems):
        self.send_sems, self.recv_sems = send_sems, recv_sems
        self.copies = []
        i, j = lax.axis_index("row"), lax.axis_index("col")
        self.x, self.core = i // 2, lax.rem(i, 2)
        self.z, self.y = j // 4, lax.rem(j, 4)
        self.i, self.j = i, j
        self.active, self.pending, self.free = [], {}, {}
        self.now, self.count = 0.0, 0

    def pos(self, axis):
        return {"x": self.x, "y": self.y, "z": self.z}[axis]

    def at(self, axis, shift):
        return lax.rem(self.pos(axis) + (shift + 4), 4)

    def peer(self, axis, shift):
        if axis == "core":
            return (self.x * 2 + 1 - self.core, self.j)
        p = self.at(axis, shift)
        if axis == "x":
            return (p * 2 + self.core, self.j)
        if axis == "y":
            return (self.i, self.z * 4 + p)
        return (self.i, p * 4 + self.y)

    def barrier(self, axes):
        sem = pltpu.get_barrier_semaphore()
        n = 0
        for axis in axes:
            for shift in (1,) if axis == "core" else (1, -1):
                pl.semaphore_signal(sem, inc=1, device_id=self.peer(axis, shift), device_id_type=MESH)
                n += 1
        pl.semaphore_wait(sem, n)

    def send(self, src, dst, axis, shift=1, level=5):
        copy = Copy(src, dst, axis, shift)
        self.count += 1
        heapq.heappush(self.pending.setdefault((axis, shift), []), (level, self.count, copy))
        return copy

    def pump(self):
        for link, heap in self.pending.items():
            while heap and self.free.get(link, 0.0) < self.now + WINDOW:
                one = heapq.heappop(heap)[2]
                k = len(self.copies)
                one.copy = pltpu.make_async_remote_copy(
                    src_ref=one.src,
                    dst_ref=one.dst,
                    send_sem=self.send_sems.at[k],
                    recv_sem=self.recv_sems.at[k],
                    device_id=self.peer(one.axis, one.shift),
                    device_id_type=MESH,
                )
                one.copy.start()
                self.copies.append(one.copy)
                end = max(self.now, self.free.get(link, 0.0)) + one.bytes / RATE[one.axis]
                self.free[link] = end
                one.arrival = end + DELAY[one.axis]

    def spawn(self, gen):
        self.active.append([gen, None])

    def run(self):
        while True:
            moved = True
            while moved:
                moved = False
                for entry in list(self.active):
                    if entry[1] is None or (callable(entry[1]) and entry[1]()):
                        moved = True
                        self.step(entry)
            self.pump()
            waits = [e for e in self.active if not callable(e[1]) and e[1].arrival is not None]
            if waits:
                entry = min(waits, key=lambda e: e[1].arrival)
                self.now = max(self.now, entry[1].arrival)
                if isinstance(entry[1], Copy):
                    entry[1].copy.wait_recv()
                self.step(entry)
            elif any(self.pending.values()):
                self.now = min(self.free.get(link, 0.0) for link, heap in self.pending.items() if heap)
            else:
                break
        assert not self.active
        for copy in self.copies:
            copy.wait_send()

    def step(self, entry):
        try:
            entry[1] = next(entry[0])
        except StopIteration:
            self.active.remove(entry)


def arrive(copy, have=None):
    yield copy
    if have is not None:
        have()


def ag_unit(net, axis, src, ref, have, way, level=5):
    p = net.at(axis, 0)
    near = net.send(src, ref(p), axis, way, level)
    other = net.send(src, ref(p), axis, -way, level)

    def chain():
        yield near
        pos = net.at(axis, -way)
        onward = net.send(ref(pos), ref(pos), axis, way, level)
        have(pos)
        yield onward
        have(net.at(axis, 2))

    net.spawn(chain())
    net.spawn(arrive(other, lambda: have(net.at(axis, way))))


def rs_unit(net, axis, part, ready, stage, emit, way, level=5, after=None):
    r, m, q = (stage(k) for k in range(3))
    box = []
    after = level if after is None else after

    def near():
        yield lambda: ready[-way]
        box.append(net.send(part(net.at(axis, -way)), q, axis, -way, level))

    def far():
        yield lambda: ready[2]
        first = net.send(part(net.at(axis, 2)), r, axis, way, level)
        yield first
        yield lambda: ready[way]
        r[...] = r[...] + part(net.at(axis, way))[...]
        yield net.send(r, m, axis, way, after)
        yield lambda: box
        yield box[0]
        yield lambda: ready[0]
        emit(part(net.at(axis, 0))[...] + (m[...] + q[...]))

    net.spawn(far())
    net.spawn(near())


ALL = {0: True, 1: True, 2: True, -1: True}
SHIFTS = (2, 1, -1, 0)
WAYS = (1, -1)


def rs_plane(net, tiles, stage_one, middle, stage_two, out, done):
    for part, (first, second) in enumerate((("z", "y"), ("y", "z"))):
        for u, way in enumerate(WAYS):
            ready = {d: False for d in SHIFTS}
            for k, d in enumerate((2, way, -way, 0)):
                pos2 = net.at(second, d)

                def term(pos1, pos2=pos2, part=part, u=u, first=first):
                    block = pos1 * 4 + pos2 if first == "z" else pos2 * 4 + pos1
                    return tiles.at[2 * block + part, pl.ds(u * 64, 64), :]

                def land(s, part=part, u=u, k=k):
                    return stage_one.at[part, k, u, s]

                def emit(value, part=part, u=u, pos2=pos2, d=d, ready=ready):
                    middle[part, pos2, u] = value
                    ready[d] = True

                rs_unit(net, first, term, ALL, land, emit, way, level=3 + k, after=2)

            def term2(pos, part=part, u=u):
                return middle.at[part, pos, u]

            def land2(s, part=part, u=u):
                return stage_two.at[part, u, s]

            def emit2(value, part=part, u=u):
                out[pl.ds(part * 128 + u * 64, 64), :] = value
                done.append((part, u))

            rs_unit(net, second, term2, ready, land2, emit2, way, level=1)


def tables_kernel(rows_ref, cols_ref, int_ref, float_ref, pad):
    pad[0:1, :] = jnp.full((1, 128), TROWS, jnp.int32)
    pad[1:2, :] = jnp.zeros((1, 128), jnp.int32)
    pad[0:1, :SLOTS] = rows_ref[...]
    pad[1:2, :SLOTS] = cols_ref[...]
    lane = lax.broadcasted_iota(jnp.int32, (128, 128), 1)
    line = lax.broadcasted_iota(jnp.int32, (128, 128), 0)

    def wide(v):
        return jnp.broadcast_to(v, (128, 128))

    def count(v):
        return jnp.sum(v, axis=0, keepdims=True)

    row, col = pad[0:1, :], pad[1:2, :]
    used = row < TROWS
    for major, minor, size, k in ((row, col, TROWS, 0), (col, row, TCOLS, 3)):
        major, minor = jnp.where(used, major, size), jnp.where(used, minor, 0)
        key = wide(major * 64 + minor)
        key_t = jnp.transpose(key)
        before = (key_t < key) | ((key_t == key) & (line < lane))
        rank_t = jnp.transpose(wide(count(before.astype(jnp.int32))))
        here = rank_t == lane
        order = count(jnp.where(here, line, 0))
        sorted_key = count(jnp.where(here, key_t, 0))
        group = sorted_key // 64
        group_t = jnp.transpose(wide(group))
        found = count((group_t == lane).astype(jnp.int32)) > 0
        last = jnp.where(found, count((group_t <= lane).astype(jnp.int32)), 0)
        int_ref[k : k + 1, :] = order
        int_ref[k + 1 : k + 2, :] = sorted_key - group * 64
        int_ref[k + 2 : k + 3, :] = last
        same = count(((group_t == wide(group)) & (line + 1 == lane)).astype(jnp.int32))
        float_ref[k : k + 1, :] = same.astype(F32)


SCRATCH = {
    "buf": ((2, CHUNK, 128, 128), F32),
    "acat": ((SLOTS, 128, 256), BF16),
    "atc": ((SLOTS, 128, 256), BF16),
    "sums_f": ((SLOTS + 1, 128, 256), F32),
    "sums_a": ((SLOTS + 1, 128, 256), F32),
    "xt": ((8, 16, 2048), F32),
    "xh": ((16, 128, 128), BF16),
    "xl": ((16, 128, 128), BF16),
    "cots": ((32, 128, 256), F32),
    "s2": ((16, 128, 256), F32),
    "fwd1": ((32, 128, 128), F32),
    "fwd2": ((32, 128, 256), F32),
    "adj": ((16, 128, 256), F32),
    "a1": ((2, 4, 2, 3, 64, 128), F32),
    "m1": ((2, 4, 2, 64, 128), F32),
    "b1": ((2, 2, 3, 64, 128), F32),
    "a2": ((2, 4, 2, 3, 64, 256), F32),
    "m2": ((2, 4, 2, 64, 256), F32),
    "b2": ((2, 2, 3, 64, 256), F32),
    "c3": ((2, 4, 128, 256), F32),
    "m3": ((2, 4, 128, 256), F32),
    "d3": ((2, 3, 128, 256), F32),
    "s": ((256, 128), F32),
    "d": ((256, 256), F32),
    "h": ((256, 256), F32),
    "p": ((256, 256), F32),
    "g": ((2, 384, 128), F32),
    "ge": ((384, 128), F32),
    "g1": ((4, 96, 128), F32),
    "gf": ((3, 96, 128), F32),
    "g2": ((4, 24, 128), F32),
    "gg": ((3, 24, 128), F32),
    "gs": ((24, 128), F32),
    "gx": ((4, 24, 128), F32),
    "gz": ((4, 24, 128), F32),
    "gy": ((4, 96, 128), F32),
    "gsib": ((4, 96, 128), F32),
}
BLOCK = 16
UNROLL = 4


def step_kernel(int_ref, float_ref, feat_ref, cot_ref, tiles_ref, win_ref, wout_ref,
                out_ref, gin_ref, gout_ref, *scratch):
    w = types.SimpleNamespace(**dict(zip(SCRATCH, scratch)))
    send_sems, recv_sems, local_sems = scratch[len(SCRATCH):]
    chunks = SLOTS // CHUNK

    def chunk_copy(k):
        return pltpu.make_async_copy(tiles_ref.at[pl.ds(k * CHUNK, CHUNK)], w.buf.at[k % 2], local_sems.at[k])

    net = Net(send_sems, recv_sems)
    loads = [chunk_copy(k) for k in range(chunks)]
    loads[0].start()
    loads[1].start()
    own_x = pltpu.make_async_copy(feat_ref, w.xt.at[net.i], local_sems.at[chunks])
    own_c = pltpu.make_async_copy(
        cot_ref, w.cots.at[pl.ds(net.j * 2, 2)], local_sems.at[chunks + 1])
    own_x.start()
    own_c.start()
    w.sums_f[0] = jnp.zeros_like(w.sums_f[0])
    w.sums_a[0] = jnp.zeros_like(w.sums_a[0])
    net.barrier(("x", "core", "y", "z"))
    seen = {"x": 0, "cot": 0, "s2": 0}
    done = {}

    def saw(name):
        seen[name] += 1

    def row_gather(name, src, ref_of, own_src, own_dst):
        for u, way in enumerate(WAYS):

            def ref(pos, u=u):
                return ref_of(pos * 2 + net.core, u)

            def have(pos, ref=ref):
                saw(name)
                net.spawn(arrive(net.send(ref(pos), ref(pos), "core"), lambda: saw(name)))

            ag_unit(net, "x", src(u), ref, have, way, 0)
        net.spawn(arrive(net.send(own_src, own_dst, "core"), lambda: saw(name)))

    def halves(u):
        return pl.ds(u * 8, 8)

    row_gather("x", lambda u: feat_ref.at[halves(u), :], lambda i, u: w.xt.at[i, halves(u), :],
               feat_ref, w.xt.at[net.i])

    for part, (first, second) in enumerate((("y", "z"), ("z", "y"))):
        for u, way in enumerate(WAYS):
            rows = pl.ds(u * 64, 64)
            src = cot_ref.at[part, rows, :]

            def ref(pos1, pos2, rows=rows, first=first, part=part):
                block = pos1 + pos2 * 4 if first == "y" else pos1 * 4 + pos2
                return w.cots.at[2 * block + part, rows, :]

            def start_second(pos1, src=None, ref=ref, second=second, way=way):
                src = ref(pos1, net.at(second, 0)) if src is None else src
                ag_unit(net, second, src, lambda pos2: ref(pos1, pos2), lambda pos: saw("cot"), way, 12)

            def have_one(pos1, start_second=start_second):
                saw("cot")
                start_second(pos1)

            ag_unit(net, first, src, lambda pos1, ref=ref, second=second: ref(pos1, net.at(second, 0)),
                    have_one, way, level=11)
            start_second(net.at(first, 0), src)

    def sums(base, k, lhs, product, store):
        def body(q, _):
            acc = None
            for v in range(UNROLL):
                n = base + q * UNROLL + v
                prev = store(n)[...] if acc is None else acc
                acc = prev * float_ref[k, n] + product(lhs[int_ref[k, n]], int_ref[k + 1, n])
                store(n + 1)[...] = acc
            return 0

        lax.fori_loop(0, BLOCK // UNROLL, body, 0)

    def pick(k, count, load, out):
        def body(r, _):
            out[r] = load(int_ref[k + 2, r])
            return 0

        lax.fori_loop(0, count, body, 0)

    def wide_product(values):
        def product(left, n):
            h, l = split(values[n])
            return dot16(left, jnp.concatenate([h, h], axis=0)) + dot16(left[:, :128], l)

        return product

    def narrow_product(left, n):
        pair = jnp.concatenate([w.xh[n], w.xl[n]], axis=1)
        res = dot16(left, jnp.concatenate([pair, pair], axis=0))
        return res[:, :128] + res[:, 128:]

    def tiles():
        for k in range(chunks):
            loads[k].wait()

            def body(n, _, k=k):
                h, l = split(w.buf[k % 2, n])
                w.acat[k * CHUNK + n] = jnp.concatenate([h, l], axis=1)
                return 0

            lax.fori_loop(0, CHUNK, body, 0)
            if k + 2 < chunks:
                loads[k + 2].start()
            yield Tick(net, 0.5, 0)
        done["acat"] = True
        for k in range(chunks):

            def turn(n, _, k=k):
                t = k * CHUNK + n
                both = w.acat[t]
                w.atc[t] = jnp.concatenate([jnp.transpose(both[:, :128]), jnp.transpose(both[:, 128:])], axis=1)
                return 0

            lax.fori_loop(0, CHUNK, turn, 0)
            yield Tick(net, 0.6, 5)
        done["atc"] = True

    def first_layer():
        yield lambda: seen["x"] == 13 and done.get("acat")
        own_x.wait()

        def split_x(c, _):
            piece = w.xt[:, :, pl.ds(pl.multiple_of(c * 128, 128), 128)].reshape(128, 128)
            h, l = split(jnp.transpose(piece))
            w.xh[c] = h
            w.xl[c] = l
            return 0

        lax.fori_loop(0, 16, split_x, 0)
        yield Tick(net, 1.0, 0)
        for base in range(0, SLOTS, BLOCK):
            sums(base, 0, w.acat, narrow_product, lambda n: w.sums_f.at[n, :, pl.ds(0, 128)])
            yield Tick(net, 1.2, 0)
        pick(0, 32, lambda n: w.sums_f[n, :, :128], w.fwd1)
        net.now += 0.5
        parts = []
        rs_plane(net, w.fwd1, w.a1, w.m1, w.b1, w.s, parts)
        yield lambda: len(parts) == 4
        pre = dot3(w.s[...], win_ref[...])
        hidden = pre * (1.0 / (1.0 + jnp.exp(-pre)))
        w.p[...] = pre
        w.h[...] = hidden
        mine = w.s2.at[pl.ds(net.i * 2, 2)]
        mine[...] = dot3(hidden, wout_ref[...]).reshape(2, 128, 256)
        net.now += 1.5
        row_gather("s2", lambda u: w.s2.at[net.i * 2 + u], lambda i, u: w.s2.at[i * 2 + u], mine, mine)
        done["pre"] = True
        yield lambda: seen["s2"] == 13
        for base in range(0, SLOTS, BLOCK):
            sums(base, 0, w.acat, wide_product(w.s2), lambda n: w.sums_f.at[n])
            yield Tick(net, 1.8, 1)
        pick(0, 32, lambda n: w.sums_f[n], w.fwd2)
        net.now += 0.8
        rs_plane(net, w.fwd2, w.a2, w.m2, w.b2, out_ref, [])

    def adjoint():
        yield lambda: seen["cot"] == 60 and done.get("atc")
        own_c.wait()
        for base in range(0, SLOTS, BLOCK):
            sums(base, 3, w.atc, wide_product(w.cots), lambda n: w.sums_a.at[n])
            yield Tick(net, 1.8, 2)
        pick(3, 16, lambda n: w.sums_a[n], w.adj)
        net.now += 0.5
        parts = []
        for u, way in enumerate(WAYS):
            ready = {d: False for d in SHIFTS}
            for k, d in enumerate((2, way, -way, 0)):
                pos = net.at("x", d)

                def cores(u=u, k=k, d=d, pos=pos, ready=ready):
                    land = w.c3.at[u, k]
                    yield net.send(w.adj.at[(pos * 2 + 1 - net.core) * 2 + u], land, "core", 1, k)
                    w.m3[u, pos] = w.adj[(pos * 2 + net.core) * 2 + u] + land[...]
                    ready[d] = True

                net.spawn(cores())

            def emit_d(value, u=u):
                w.d[pl.ds(u * 128, 128), :] = value
                parts.append(u)

            rs_unit(net, "x", lambda pos, u=u: w.m3.at[u, pos], ready, lambda k, u=u: w.d3.at[u, k], emit_d, way)
        yield lambda: len(parts) == 2 and done.get("pre")
        net.pump()
        d = w.d[...]
        pre = w.p[...]
        sg = 1.0 / (1.0 + jnp.exp(-pre))
        d_pre = dot3(d, wout_ref[...], (((1,), (1,)), ((), ()))) * sg * (1.0 + pre * (1.0 - sg))
        grad_in = dot3(jnp.transpose(w.s[...]), d_pre)
        grad_out = dot3(jnp.transpose(w.h[...]), d)
        for c in range(2):
            lanes = slice(c * 128, c * 128 + 128)
            w.g[c, pl.ds(0, 128), :] = grad_in[:, lanes]
            w.g[c, pl.ds(128, 256), :] = grad_out[:, lanes]
        net.now += 2.0
        yield net.send(w.g.at[1 - net.core], w.ge, "core", 1, 0)
        w.g1[...] = (w.g[net.core] + w.ge[...]).reshape(w.g1.shape)
        one, two = [], []

        def emit_one(value):
            w.g2[...] = value.reshape(w.g2.shape)
            one.append(0)

        rs_unit(net, "y", lambda pos: w.g1.at[pos], ALL, lambda k: w.gf.at[k], emit_one, 1, 0)
        yield lambda: one

        def emit_two(value):
            w.gs[...] = value
            two.append(0)

        rs_unit(net, "z", lambda pos: w.g2.at[pos], ALL, lambda k: w.gg.at[k], emit_two, 1, 0)
        yield lambda: two

        def walk(axis, src, dst):
            got = []
            ag_unit(net, axis, src, lambda pos: dst.at[pos], got.append, 1, 0)
            yield lambda: len(got) == 3

        w.gx[net.x] = w.gs[...]
        yield from walk("x", w.gs, w.gx)
        w.gz[net.z] = (w.gx[0] + w.gx[1]) + (w.gx[2] + w.gx[3])
        yield from walk("z", w.gz.at[net.z], w.gz)
        w.gy[net.y] = w.gz[...].reshape(96, 128)
        yield from walk("y", w.gy.at[net.y], w.gy)
        yield net.send(w.gy, w.gsib, "core", 1, 0)
        mine, other = w.gy[...].reshape(384, 128), w.gsib[...].reshape(384, 128)
        first = net.core == 0
        low = jnp.where(first, mine, other)
        high = jnp.where(first, other, mine)
        gin_ref[:, :128] = low[:128]
        gin_ref[:, 128:] = high[:128]
        gout_ref[:, :128] = low[128:]
        gout_ref[:, 128:] = high[128:]

    net.spawn(tiles())
    net.spawn(first_layer())
    net.spawn(adjoint())
    net.run()


def finish_kernel(a_ref, b_ref, c_ref, out_a, out_b, out_c):
    out_a[...] = a_ref[...]
    out_b[...] = b_ref[...]
    out_c[...] = c_ref[...]


ANY = pl.BlockSpec(memory_space=pl.ANY)
VM = pl.BlockSpec(memory_space=pltpu.VMEM)
SM = pl.BlockSpec(memory_space=pltpu.SMEM)


def shape(*dims, kind=F32):
    return jax.ShapeDtypeStruct(dims, kind)


def per_device(features, tile_rows, tile_cols, tile_values, weight_in, weight_out, cotangent):
    ints, floats = pl.pallas_call(
        tables_kernel,
        out_shape=(shape(8, 128, kind=jnp.int32), shape(8, 128)),
        in_specs=[VM, VM],
        out_specs=(VM, VM),
        scratch_shapes=[pltpu.VMEM((8, 128), jnp.int32)],
        name="tables",
    )(tile_rows.reshape(1, SLOTS), tile_cols.reshape(1, SLOTS))
    outs_shape = (shape(256, 256), shape(128, 256), shape(256, 256))
    outs = pl.pallas_call(
        step_kernel,
        out_shape=outs_shape,
        in_specs=[SM, SM, ANY, ANY, ANY, VM, VM],
        out_specs=(VM, VM, VM),
        scratch_shapes=[pltpu.VMEM(dims, kind) for dims, kind in SCRATCH.values()]
        + [
            pltpu.SemaphoreType.DMA((COPIES,)),
            pltpu.SemaphoreType.DMA((COPIES,)),
            pltpu.SemaphoreType.DMA((SLOTS // CHUNK + 2,)),
        ],
        compiler_params=pltpu.CompilerParams(
            collective_id=0, has_side_effects=True, vmem_limit_bytes=VMEM_LIMIT),
        name="step",
    )(ints, floats, features.T, cotangent.reshape(2, 128, 256), tile_values.reshape(SLOTS, 128, 128),
      weight_in, weight_out)
    return pl.pallas_call(
        finish_kernel, out_shape=outs_shape, in_specs=[VM] * 3, out_specs=(VM,) * 3, name="finish",
    )(*outs)


def solution(mesh):
    return jax.shard_map(
        per_device,
        mesh=mesh,
        in_specs=(
            P("col", "row"),
            P("row", "col", None),
            P("row", "col", None),
            P("row", "col", None, None, None),
            P(),
            P(),
            P(("col", "row"), None),
        ),
        out_specs=(P(("col", "row"), None), P(), P()),
        check_vma=False,
    )
```

time: 652 us -> 117 us (0.18); the launches traced: 642 us -> 115 us
  waiting for transfers between devices: 382 us -> 0 us
  matrix products: 128 us -> 0 us
  Pallas kernels: 0 us -> 114 us
  local copies, waits for them, and re-layouts: 105 us -> 0 us
  between operations: 14.4 us -> 0.64 us
  blocking collectives: 10.3 us -> 0 us
    reduce_scatter x4 -> x0, waiting for transfers between devices: 157 us -> none  [the longest x1 79 us: per_device(): lax.psum_scatter(partial_two, 'col', scatter_dimension=0, tiled=True)]
    psum x1 -> x0, waiting for transfers between devices: 134 us -> none  [per_device(): lax.psum((grad_in_local, grad_out_local), ('row', 'col'))]
    dot_general x13 -> x0, matrix products: 128 us -> none  [the longest x2 46.4 us: adjoint_tiles(): jnp.einsum('tba,tbf->taf', tile_block, picked, precision=lax.Precision.HI...]
    pallas_call x0 -> x3, Pallas kernels: none -> 114 us  [the longest x1 111 us: per_device(): pl.pallas_call(step_kernel, out_shape=outs_shape, in_specs=[SM, SM, ANY,...]
    all_gather x4 -> x0, waiting for transfers between devices: 91.1 us -> none  [the longest x1 48.8 us: per_device(): rows_in = lax.all_gather(d_pre, 'col', axis=0, tiled=True)]
    dot_general x8 -> x0, local copies, waits for them, and re-layouts: 60.5 us -> none  [the longest x2 23.3 us: forward_tiles(): jnp.einsum('tab,tbf->taf', tile_block, picked, precision=lax.Precision.HI...]
    gather x4 -> x0, local copies, waits for them, and re-layouts: 40.4 us -> none  [the longest x2 20.9 us: adjoint_tiles(): picked = jnp.take(blocks, jnp.minimum(tile_row, in_tiles - 1), axis=0)]
    all_to_all x1 -> x0, blocking collectives: 10.3 us -> none  [per_device(): lax.all_to_all(features, 'row', split_axis=0, concat_axis=1, tiled=True)]
  transfers between devices with their start and end apart: 9 -> 0, of which waited for: 5 -> 0; matrix products, arithmetic and copies ran while one was open for 36% -> 0% of each run, Pallas kernels for 0% -> 0%
where the time goes in v3:
time: 117 us; the launch traced here: 115 us
  Pallas kernels  114 us (97%)
    pallas_call x1, Pallas kernels, per_device(): pl.pallas_call(step_kernel, out_shape=outs_shape, in_specs=[SM, SM, ANY,...  111 us

profile of v3, /device:TPU:0, one launch (start us, length us, event | category | flops | bytes accessed | tf_op | source)
XLA Modules:
  0.0 114.8 jit_solution(1633708076261227399)
XLA Ops:
  0.6 1.6 %tables.1 = (s32[8,128]{1,0:T(8,128)}, f32[8,128]{1,0:T(8,128)}) custom-call(s32[1,80]{1,0:T(1,128)} %bitcast.8, s32[1,80]{1,0:T(1,128)} %bitcast.9), custom_call_target="tpu_custom_call" | custom-call | tf_op jit(solution)/shard_map/tables/pallas_call | solution.py:580
  2.3 110.6 %step.1 = (f32[256,256]{1,0:T(8,128)}, f32[128,256]{1,0:T(8,128)}, f32[256,256]{1,0:T(8,128)}) custom-call(s32[8,128]{1,0:T(8,128)} %get-tuple-element.8.int_ref, f32[8,128]{1,0:T(8,128)} %get-tuple-element.9.float_ref, f32[16,2048]{1,0:T(8,128)} %bitcast.7, f32[2,128,256]{2,1,0:T(8,128)} %bitcast.6, f32[80,128,128]{2,1,0:T(8,128)} %bitcast.5, ...), custom_call_target="tpu_custom_call" | custom-call | tf_op jit(solution)/shard_map/step/pallas_call | solution.py:589
  112.8 1.9 %finish.1 = (f32[256,256]{1,0:T(8,128)}, f32[128,256]{1,0:T(8,128)}, f32[256,256]{1,0:T(8,128)}) custom-call(f32[256,256]{1,0:T(8,128)} %get-tuple-element.10.a_ref, f32[128,256]{1,0:T(8,128)} %get-tuple-element.11.b_ref, f32[256,256]{1,0:T(8,128)} %get-tuple-element.12.c_ref), custom_call_target="tpu_custom_call" | custom-call | tf_op jit(solution)/shard_map/finish/pallas_call | solution.py:605

commit v4 on v3

--- a/solution.py
+++ b/solution.py
@@ -17,7 +17,7 @@
 SLOTS = 80
 TROWS = 32
 TCOLS = 16
-COPIES = 240
+COPIES = 320
 
 
 def split(v):
@@ -44,7 +44,7 @@
 
 RATE = {"x": 45e3, "y": 45e3, "z": 45e3, "core": 250e3}
 DELAY = {"x": 1.6, "y": 1.6, "z": 1.6, "core": 1.0}
-WINDOW = 2.5
+WINDOW = 1.5
 
 
 class Tick:
@@ -84,7 +84,7 @@
         sem = pltpu.get_barrier_semaphore()
         n = 0
         for axis in axes:
-            for shift in (1,) if axis == "core" else (1, -1):
+            for shift in (1,) if axis == "core" else (1, -1, 2):
                 pl.semaphore_signal(sem, inc=1, device_id=self.peer(axis, shift), device_id_type=MESH)
                 n += 1
         pl.semaphore_wait(sem, n)
@@ -92,7 +92,8 @@
     def send(self, src, dst, axis, shift=1, level=5):
         copy = Copy(src, dst, axis, shift)
         self.count += 1
-        heapq.heappush(self.pending.setdefault((axis, shift), []), (level, self.count, copy))
+        link = (axis, 1 if shift == 2 else shift)
+        heapq.heappush(self.pending.setdefault(link, []), (level, self.count, copy))
         return copy
 
     def pump(self):
@@ -112,7 +113,7 @@
                 self.copies.append(one.copy)
                 end = max(self.now, self.free.get(link, 0.0)) + one.bytes / RATE[one.axis]
                 self.free[link] = end
-                one.arrival = end + DELAY[one.axis]
+                one.arrival = end + DELAY[one.axis] * (1.5 if one.shift == 2 else 1)
 
     def spawn(self, gen):
         self.active.append([gen, None])
@@ -136,6 +137,7 @@
                 self.step(entry)
             elif any(self.pending.values()):
                 self.now = min(self.free.get(link, 0.0) for link, heap in self.pending.items() if heap)
+                self.now -= WINDOW / 2
             else:
                 break
         assert not self.active
@@ -197,12 +199,24 @@
     net.spawn(near())
 
 
+def gather_direct(net, axis, src, dst, level=0):
+    copies = [net.send(src, dst.at[net.at(axis, 0)], axis, d, level) for d in (2, 1, -1)]
+    for copy in copies[1:] + copies[:1]:
+        yield copy
+
+
+def reduce_direct(net, axis, terms, land, level=0):
+    copies = [net.send(terms.at[net.at(axis, d)], land.at[k], axis, d, level) for k, d in enumerate((2, 1, -1))]
+    for copy in copies[1:] + copies[:1]:
+        yield copy
+
+
 ALL = {0: True, 1: True, 2: True, -1: True}
 SHIFTS = (2, 1, -1, 0)
 WAYS = (1, -1)
 
 
-def rs_plane(net, tiles, stage_one, middle, stage_two, out, done):
+def rs_plane(net, tiles, stage_one, middle, stage_two, out, done, lanes=slice(None), base=0):
     for part, (first, second) in enumerate((("z", "y"), ("y", "z"))):
         for u, way in enumerate(WAYS):
             ready = {d: False for d in SHIFTS}
@@ -220,7 +234,7 @@
                     middle[part, pos2, u] = value
                     ready[d] = True
 
-                rs_unit(net, first, term, ALL, land, emit, way, level=3 + k, after=2)
+                rs_unit(net, first, term, ALL, land, emit, way, level=base + 3 + k, after=base + 2)
 
             def term2(pos, part=part, u=u):
                 return middle.at[part, pos, u]
@@ -229,10 +243,10 @@
                 return stage_two.at[part, u, s]
 
             def emit2(value, part=part, u=u):
-                out[pl.ds(part * 128 + u * 64, 64), :] = value
+                out[part * 128 + u * 64 : part * 128 + u * 64 + 64, lanes] = value
                 done.append((part, u))
 
-            rs_unit(net, second, term2, ready, land2, emit2, way, level=1)
+            rs_unit(net, second, term2, ready, land2, emit2, way, level=base + 1)
 
 
 def tables_kernel(rows_ref, cols_ref, int_ref, float_ref, pad):
@@ -275,22 +289,23 @@
     "buf": ((2, CHUNK, 128, 128), F32),
     "acat": ((SLOTS, 128, 256), BF16),
     "atc": ((SLOTS, 128, 256), BF16),
-    "sums_f": ((SLOTS + 1, 128, 256), F32),
+    "sums_f": ((SLOTS + 1, 128, 128), F32),
     "sums_a": ((SLOTS + 1, 128, 256), F32),
     "xt": ((8, 16, 2048), F32),
     "xh": ((16, 128, 128), BF16),
     "xl": ((16, 128, 128), BF16),
     "cots": ((32, 128, 256), F32),
-    "s2": ((16, 128, 256), F32),
+    "s2_0": ((16, 128, 128), F32),
+    "s2_1": ((16, 128, 128), F32),
     "fwd1": ((32, 128, 128), F32),
-    "fwd2": ((32, 128, 256), F32),
+    "fwd2": ((2, 32, 128, 128), F32),
     "adj": ((16, 128, 256), F32),
     "a1": ((2, 4, 2, 3, 64, 128), F32),
     "m1": ((2, 4, 2, 64, 128), F32),
     "b1": ((2, 2, 3, 64, 128), F32),
-    "a2": ((2, 4, 2, 3, 64, 256), F32),
-    "m2": ((2, 4, 2, 64, 256), F32),
-    "b2": ((2, 2, 3, 64, 256), F32),
+    "a2": ((2, 2, 4, 2, 3, 64, 128), F32),
+    "m2": ((2, 2, 4, 2, 64, 128), F32),
+    "b2": ((2, 2, 2, 3, 64, 128), F32),
     "c3": ((2, 4, 128, 256), F32),
     "m3": ((2, 4, 128, 256), F32),
     "d3": ((2, 3, 128, 256), F32),
@@ -302,15 +317,13 @@
     "ge": ((384, 128), F32),
     "g1": ((4, 96, 128), F32),
     "gf": ((3, 96, 128), F32),
-    "g2": ((4, 24, 128), F32),
-    "gg": ((3, 24, 128), F32),
-    "gs": ((24, 128), F32),
-    "gx": ((4, 24, 128), F32),
-    "gz": ((4, 24, 128), F32),
+    "gs": ((96, 128), F32),
+    "g2": ((4, 96, 128), F32),
+    "gz": ((4, 96, 128), F32),
     "gy": ((4, 96, 128), F32),
     "gsib": ((4, 96, 128), F32),
 }
-BLOCK = 16
+BLOCK = 8
 UNROLL = 4
 
 
@@ -335,13 +348,13 @@
     w.sums_f[0] = jnp.zeros_like(w.sums_f[0])
     w.sums_a[0] = jnp.zeros_like(w.sums_a[0])
     net.barrier(("x", "core", "y", "z"))
-    seen = {"x": 0, "cot": 0, "s2": 0}
+    seen = {"x": 0, "cot": 0, 0: 0, 1: 0}
     done = {}
 
     def saw(name):
         seen[name] += 1
 
-    def row_gather(name, src, ref_of, own_src, own_dst):
+    def row_gather(name, src, ref_of, own_src, own_dst, level=0):
         for u, way in enumerate(WAYS):
 
             def ref(pos, u=u):
@@ -351,7 +364,7 @@
                 saw(name)
                 net.spawn(arrive(net.send(ref(pos), ref(pos), "core"), lambda: saw(name)))
 
-            ag_unit(net, "x", src(u), ref, have, way, 0)
+            ag_unit(net, "x", src(u), ref, have, way, level)
         net.spawn(arrive(net.send(own_src, own_dst, "core"), lambda: saw(name)))
 
     def halves(u):
@@ -371,14 +384,14 @@
 
             def start_second(pos1, src=None, ref=ref, second=second, way=way):
                 src = ref(pos1, net.at(second, 0)) if src is None else src
-                ag_unit(net, second, src, lambda pos2: ref(pos1, pos2), lambda pos: saw("cot"), way, 12)
+                ag_unit(net, second, src, lambda pos2: ref(pos1, pos2), lambda pos: saw("cot"), way, -1)
 
             def have_one(pos1, start_second=start_second):
                 saw("cot")
                 start_second(pos1)
 
             ag_unit(net, first, src, lambda pos1, ref=ref, second=second: ref(pos1, net.at(second, 0)),
-                    have_one, way, level=11)
+                    have_one, way, level=-2)
             start_second(net.at(first, 0), src)
 
     def sums(base, k, lhs, product, store):
@@ -407,8 +420,8 @@
 
         return product
 
-    def narrow_product(left, n):
-        pair = jnp.concatenate([w.xh[n], w.xl[n]], axis=1)
+    def narrow(left, h, l):
+        pair = jnp.concatenate([h, l], axis=1)
         res = dot16(left, jnp.concatenate([pair, pair], axis=0))
         return res[:, :128] + res[:, 128:]
 
@@ -452,9 +465,9 @@
         lax.fori_loop(0, 16, split_x, 0)
         yield Tick(net, 1.0, 0)
         for base in range(0, SLOTS, BLOCK):
-            sums(base, 0, w.acat, narrow_product, lambda n: w.sums_f.at[n, :, pl.ds(0, 128)])
-            yield Tick(net, 1.2, 0)
-        pick(0, 32, lambda n: w.sums_f[n, :, :128], w.fwd1)
+            sums(base, 0, w.acat, lambda left, n: narrow(left, w.xh[n], w.xl[n]), lambda n: w.sums_f.at[n])
+            yield Tick(net, 0.6, 0)
+        pick(0, 32, lambda n: w.sums_f[n], w.fwd1)
         net.now += 0.5
         parts = []
         rs_plane(net, w.fwd1, w.a1, w.m1, w.b1, w.s, parts)
@@ -463,25 +476,31 @@
         hidden = pre * (1.0 / (1.0 + jnp.exp(-pre)))
         w.p[...] = pre
         w.h[...] = hidden
-        mine = w.s2.at[pl.ds(net.i * 2, 2)]
-        mine[...] = dot3(hidden, wout_ref[...]).reshape(2, 128, 256)
-        net.now += 1.5
-        row_gather("s2", lambda u: w.s2.at[net.i * 2 + u], lambda i, u: w.s2.at[i * 2 + u], mine, mine)
+        for f in range(2):
+            s2 = (w.s2_0, w.s2_1)[f]
+            mine = s2.at[pl.ds(net.i * 2, 2)]
+            mine[...] = dot3(hidden, wout_ref[:, f * 128 : f * 128 + 128]).reshape(2, 128, 128)
+            net.now += 0.6
+            row_gather(f, lambda u, s2=s2: s2.at[net.i * 2 + u], lambda i, u, s2=s2: s2.at[i * 2 + u], mine, mine, f)
+            net.pump()
         done["pre"] = True
-        yield lambda: seen["s2"] == 13
-        for base in range(0, SLOTS, BLOCK):
-            sums(base, 0, w.acat, wide_product(w.s2), lambda n: w.sums_f.at[n])
-            yield Tick(net, 1.8, 1)
-        pick(0, 32, lambda n: w.sums_f[n], w.fwd2)
-        net.now += 0.8
-        rs_plane(net, w.fwd2, w.a2, w.m2, w.b2, out_ref, [])
+        for f in range(2):
+            yield lambda: seen[f] == 13
+            s2 = (w.s2_0, w.s2_1)[f]
+            for base in range(0, SLOTS, BLOCK):
+                sums(base, 0, w.acat, lambda left, n: narrow(left, *split(s2[n])), lambda n: w.sums_f.at[n])
+                yield Tick(net, 0.6, 1)
+            pick(0, 32, lambda n: w.sums_f[n], w.fwd2.at[f])
+            net.now += 0.5
+            rs_plane(net, w.fwd2.at[f], w.a2.at[f], w.m2.at[f], w.b2.at[f], out_ref, [],
+                     slice(f * 128, f * 128 + 128), 6 * f)
 
     def adjoint():
         yield lambda: seen["cot"] == 60 and done.get("atc")
         own_c.wait()
         for base in range(0, SLOTS, BLOCK):
             sums(base, 3, w.atc, wide_product(w.cots), lambda n: w.sums_a.at[n])
-            yield Tick(net, 1.8, 2)
+            yield Tick(net, 0.9, 2)
         pick(3, 16, lambda n: w.sums_a[n], w.adj)
         net.now += 0.5
         parts = []
@@ -502,7 +521,7 @@
                 w.d[pl.ds(u * 128, 128), :] = value
                 parts.append(u)
 
-            rs_unit(net, "x", lambda pos, u=u: w.m3.at[u, pos], ready, lambda k, u=u: w.d3.at[u, k], emit_d, way)
+            rs_unit(net, "x", lambda pos, u=u: w.m3.at[u, pos], ready, lambda k, u=u: w.d3.at[u, k], emit_d, way, 0.5)
         yield lambda: len(parts) == 2 and done.get("pre")
         net.pump()
         d = w.d[...]
@@ -518,33 +537,18 @@
         net.now += 2.0
         yield net.send(w.g.at[1 - net.core], w.ge, "core", 1, 0)
         w.g1[...] = (w.g[net.core] + w.ge[...]).reshape(w.g1.shape)
-        one, two = [], []
-
-        def emit_one(value):
-            w.g2[...] = value.reshape(w.g2.shape)
-            one.append(0)
-
-        rs_unit(net, "y", lambda pos: w.g1.at[pos], ALL, lambda k: w.gf.at[k], emit_one, 1, 0)
-        yield lambda: one
-
-        def emit_two(value):
-            w.gs[...] = value
-            two.append(0)
-
-        rs_unit(net, "z", lambda pos: w.g2.at[pos], ALL, lambda k: w.gg.at[k], emit_two, 1, 0)
-        yield lambda: two
-
-        def walk(axis, src, dst):
-            got = []
-            ag_unit(net, axis, src, lambda pos: dst.at[pos], got.append, 1, 0)
-            yield lambda: len(got) == 3
-
-        w.gx[net.x] = w.gs[...]
-        yield from walk("x", w.gs, w.gx)
-        w.gz[net.z] = (w.gx[0] + w.gx[1]) + (w.gx[2] + w.gx[3])
-        yield from walk("z", w.gz.at[net.z], w.gz)
-        w.gy[net.y] = w.gz[...].reshape(96, 128)
-        yield from walk("y", w.gy.at[net.y], w.gy)
+
+        def total(terms, own, land):
+            return (terms[own] + land[0]) + (land[1] + land[2])
+
+        yield from reduce_direct(net, "x", w.g1, w.gf)
+        w.gs[...] = total(w.g1, net.x, w.gf)
+        for axis, land in (("y", w.g2), ("z", w.gz)):
+            land[net.pos(axis)] = w.gs[...]
+            yield from gather_direct(net, axis, land.at[net.pos(axis)], land)
+            w.gs[...] = (land[0] + land[1]) + (land[2] + land[3])
+        w.gy[net.x] = w.gs[...]
+        yield from gather_direct(net, "x", w.gs, w.gy)
         yield net.send(w.gy, w.gsib, "core", 1, 0)
         mine, other = w.gy[...].reshape(384, 128), w.gsib[...].reshape(384, 128)
         first = net.core == 0

time: 117 us -> 108 us (0.923); the launches traced: 115 us -> 107 us
  Pallas kernels: 114 us -> 106 us
    pallas_call x1, Pallas kernels: 111 us -> 103 us  [per_device(): pl.pallas_call(step_kernel, out_shape=outs_shape, in_specs=[SM, SM, ANY,...]
where the time goes in v4:
time: 108 us; the launch traced here: 107 us
  Pallas kernels  106 us (98%)
    pallas_call x1, Pallas kernels, per_device(): pl.pallas_call(step_kernel, out_shape=outs_shape, in_specs=[SM, SM, ANY,...  103 us

profile of v4, /device:TPU:0, one launch (start us, length us, event | category | flops | bytes accessed | tf_op | source)
XLA Modules:
  0.0 107.1 jit_solution(8768150737043568482)
XLA Ops:
  0.6 1.6 %tables.1 = (s32[8,128]{1,0:T(8,128)}, f32[8,128]{1,0:T(8,128)}) custom-call(s32[1,80]{1,0:T(1,128)} %bitcast.8, s32[1,80]{1,0:T(1,128)} %bitcast.9), custom_call_target="tpu_custom_call" | custom-call | tf_op jit(solution)/shard_map/tables/pallas_call | solution.py:584
  2.3 102.9 %step.1 = (f32[256,256]{1,0:T(8,128)}, f32[128,256]{1,0:T(8,128)}, f32[256,256]{1,0:T(8,128)}) custom-call(s32[8,128]{1,0:T(8,128)} %get-tuple-element.8.int_ref, f32[8,128]{1,0:T(8,128)} %get-tuple-element.9.float_ref, f32[16,2048]{1,0:T(8,128)} %bitcast.7, f32[2,128,256]{2,1,0:T(8,128)} %bitcast.6, f32[80,128,128]{2,1,0:T(8,128)} %bitcast.5, ...), custom_call_target="tpu_custom_call" | custom-call | tf_op jit(solution)/shard_map/step/pallas_call | solution.py:593
  105.1 1.9 %finish.1 = (f32[256,256]{1,0:T(8,128)}, f32[128,256]{1,0:T(8,128)}, f32[256,256]{1,0:T(8,128)}) custom-call(f32[256,256]{1,0:T(8,128)} %get-tuple-element.10.a_ref, f32[128,256]{1,0:T(8,128)} %get-tuple-element.11.b_ref, f32[256,256]{1,0:T(8,128)} %get-tuple-element.12.c_ref), custom_call_target="tpu_custom_call" | custom-call | tf_op jit(solution)/shard_map/finish/pallas_call | solution.py:609

commit v5 on v4

--- a/solution.py
+++ b/solution.py
@@ -17,7 +17,8 @@
 SLOTS = 80
 TROWS = 32
 TCOLS = 16
-COPIES = 320
+COPIES = 307
+SIZES = tuple(k * 1024 for k in (32, 48, 64, 128, 192))
 
 
 def split(v):
@@ -44,7 +45,7 @@
 
 RATE = {"x": 45e3, "y": 45e3, "z": 45e3, "core": 250e3}
 DELAY = {"x": 1.6, "y": 1.6, "z": 1.6, "core": 1.0}
-WINDOW = 1.5
+WINDOW = 3.0
 
 
 class Tick:
@@ -56,7 +57,7 @@
 class Net:
     def __init__(self, send_sems, recv_sems):
         self.send_sems, self.recv_sems = send_sems, recv_sems
-        self.copies = []
+        self.copies, self.sent = [], {}
         i, j = lax.axis_index("row"), lax.axis_index("col")
         self.x, self.core = i // 2, lax.rem(i, 2)
         self.z, self.y = j // 4, lax.rem(j, 4)
@@ -104,13 +105,14 @@
                 one.copy = pltpu.make_async_remote_copy(
                     src_ref=one.src,
                     dst_ref=one.dst,
-                    send_sem=self.send_sems.at[k],
+                    send_sem=self.send_sems.at[SIZES.index(one.bytes)],
                     recv_sem=self.recv_sems.at[k],
                     device_id=self.peer(one.axis, one.shift),
                     device_id_type=MESH,
                 )
                 one.copy.start()
                 self.copies.append(one.copy)
+                self.sent[one.bytes] = self.sent.get(one.bytes, 0) + one.bytes
                 end = max(self.now, self.free.get(link, 0.0)) + one.bytes / RATE[one.axis]
                 self.free[link] = end
                 one.arrival = end + DELAY[one.axis] * (1.5 if one.shift == 2 else 1)
@@ -118,7 +120,7 @@
     def spawn(self, gen):
         self.active.append([gen, None])
 
-    def run(self):
+    def run(self, whole):
         while True:
             moved = True
             while moved:
@@ -141,8 +143,19 @@
             else:
                 break
         assert not self.active
-        for copy in self.copies:
-            copy.wait_send()
+        assert len(self.copies) == COPIES
+        for size, total in self.sent.items():
+            unit = 128 if total % (128 * 1024) == 0 else 64
+            span = whole[unit].at[pl.ds(0, total // (unit * 1024))]
+            assert 4 * math.prod(span.shape) * (1 if unit == 128 else 0.5) == total
+            pltpu.make_async_remote_copy(
+                src_ref=span,
+                dst_ref=span,
+                send_sem=self.send_sems.at[SIZES.index(size)],
+                recv_sem=self.recv_sems.at[0],
+                device_id=self.peer("core", 1),
+                device_id_type=MESH,
+            ).wait_send()
 
     def step(self, entry):
         try:
@@ -286,7 +299,7 @@
 
 
 SCRATCH = {
-    "buf": ((2, CHUNK, 128, 128), F32),
+    "buf": ((SLOTS, 128, 128), F32),
     "acat": ((SLOTS, 128, 256), BF16),
     "atc": ((SLOTS, 128, 256), BF16),
     "sums_f": ((SLOTS + 1, 128, 128), F32),
@@ -334,17 +347,17 @@
     chunks = SLOTS // CHUNK
 
     def chunk_copy(k):
-        return pltpu.make_async_copy(tiles_ref.at[pl.ds(k * CHUNK, CHUNK)], w.buf.at[k % 2], local_sems.at[k])
+        return pltpu.make_async_copy(tiles_ref.at[pl.ds(k * CHUNK, CHUNK)], w.buf.at[pl.ds(k * CHUNK, CHUNK)], local_sems.at[k])
 
     net = Net(send_sems, recv_sems)
     loads = [chunk_copy(k) for k in range(chunks)]
-    loads[0].start()
-    loads[1].start()
     own_x = pltpu.make_async_copy(feat_ref, w.xt.at[net.i], local_sems.at[chunks])
     own_c = pltpu.make_async_copy(
         cot_ref, w.cots.at[pl.ds(net.j * 2, 2)], local_sems.at[chunks + 1])
     own_x.start()
     own_c.start()
+    for load in loads:
+        load.start()
     w.sums_f[0] = jnp.zeros_like(w.sums_f[0])
     w.sums_a[0] = jnp.zeros_like(w.sums_a[0])
     net.barrier(("x", "core", "y", "z"))
@@ -430,13 +443,11 @@
             loads[k].wait()
 
             def body(n, _, k=k):
-                h, l = split(w.buf[k % 2, n])
+                h, l = split(w.buf[k * CHUNK + n])
                 w.acat[k * CHUNK + n] = jnp.concatenate([h, l], axis=1)
                 return 0
 
             lax.fori_loop(0, CHUNK, body, 0)
-            if k + 2 < chunks:
-                loads[k + 2].start()
             yield Tick(net, 0.5, 0)
         done["acat"] = True
         for k in range(chunks):
@@ -562,7 +573,7 @@
     net.spawn(tiles())
     net.spawn(first_layer())
     net.spawn(adjoint())
-    net.run()
+    net.run({64: w.acat, 128: w.sums_a})
 
 
 def finish_kernel(a_ref, b_ref, c_ref, out_a, out_b, out_c):
@@ -597,7 +608,7 @@
         out_specs=(VM, VM, VM),
         scratch_shapes=[pltpu.VMEM(dims, kind) for dims, kind in SCRATCH.values()]
         + [
-            pltpu.SemaphoreType.DMA((COPIES,)),
+            pltpu.SemaphoreType.DMA((len(SIZES),)),
             pltpu.SemaphoreType.DMA((COPIES,)),
             pltpu.SemaphoreType.DMA((SLOTS // CHUNK + 2,)),
         ],

time: 108 us -> 99.8 us (0.924)
  Pallas kernels: 106 us -> 99 us
    pallas_call x1, Pallas kernels: 103 us -> 95.5 us  [per_device(): pl.pallas_call(step_kernel, out_shape=outs_shape, in_specs=[SM, SM, ANY,...]
where the time goes in v5:
time: 99.8 us; the launch traced here: 99.7 us
  Pallas kernels  99 us (99%)
    pallas_call x1, Pallas kernels, per_device(): pl.pallas_call(step_kernel, out_shape=outs_shape, in_specs=[SM, SM, ANY,...  95.5 us

profile of v5, /device:TPU:0, one launch (start us, length us, event | category | flops | bytes accessed | tf_op | source)
XLA Modules:
  0.0 99.7 jit_solution(2475162834159070907)
XLA Ops:
  0.6 1.6 %tables.1 = (s32[8,128]{1,0:T(8,128)}, f32[8,128]{1,0:T(8,128)}) custom-call(s32[1,80]{1,0:T(1,128)} %bitcast.8, s32[1,80]{1,0:T(1,128)} %bitcast.9), custom_call_target="tpu_custom_call" | custom-call | tf_op jit(solution)/shard_map/tables/pallas_call | solution.py:595
  2.3 95.5 %step.1 = (f32[256,256]{1,0:T(8,128)}, f32[128,256]{1,0:T(8,128)}, f32[256,256]{1,0:T(8,128)}) custom-call(s32[8,128]{1,0:T(8,128)} %get-tuple-element.8.int_ref, f32[8,128]{1,0:T(8,128)} %get-tuple-element.9.float_ref, f32[16,2048]{1,0:T(8,128)} %bitcast.7, f32[2,128,256]{2,1,0:T(8,128)} %bitcast.6, f32[80,128,128]{2,1,0:T(8,128)} %bitcast.5, ...), custom_call_target="tpu_custom_call" | custom-call | tf_op jit(solution)/shard_map/step/pallas_call | solution.py:604
  97.7 1.9 %finish.1 = (f32[256,256]{1,0:T(8,128)}, f32[128,256]{1,0:T(8,128)}, f32[256,256]{1,0:T(8,128)}) custom-call(f32[256,256]{1,0:T(8,128)} %get-tuple-element.10.a_ref, f32[128,256]{1,0:T(8,128)} %get-tuple-element.11.b_ref, f32[256,256]{1,0:T(8,128)} %get-tuple-element.12.c_ref), custom_call_target="tpu_custom_call" | custom-call | tf_op jit(solution)/shard_map/finish/pallas_call | solution.py:620

commit v6 on v5

--- a/solution.py
+++ b/solution.py
@@ -322,6 +322,8 @@
     "c3": ((2, 4, 128, 256), F32),
     "m3": ((2, 4, 128, 256), F32),
     "d3": ((2, 3, 128, 256), F32),
+    "win": ((128, 256), F32),
+    "wout": ((256, 256), F32),
     "s": ((256, 128), F32),
     "d": ((256, 256), F32),
     "h": ((256, 256), F32),
@@ -336,7 +338,7 @@
     "gy": ((4, 96, 128), F32),
     "gsib": ((4, 96, 128), F32),
 }
-BLOCK = 8
+BLOCK = 4
 UNROLL = 4
 
 
@@ -354,6 +356,12 @@
     own_x = pltpu.make_async_copy(feat_ref, w.xt.at[net.i], local_sems.at[chunks])
     own_c = pltpu.make_async_copy(
         cot_ref, w.cots.at[pl.ds(net.j * 2, 2)], local_sems.at[chunks + 1])
+    weights = [
+        pltpu.make_async_copy(win_ref, w.win, local_sems.at[chunks + 2]),
+        pltpu.make_async_copy(wout_ref, w.wout, local_sems.at[chunks + 3]),
+    ]
+    for weight in weights:
+        weight.start()
     own_x.start()
     own_c.start()
     for load in loads:
@@ -477,20 +485,22 @@
         yield Tick(net, 1.0, 0)
         for base in range(0, SLOTS, BLOCK):
             sums(base, 0, w.acat, lambda left, n: narrow(left, w.xh[n], w.xl[n]), lambda n: w.sums_f.at[n])
-            yield Tick(net, 0.6, 0)
+            yield Tick(net, 0.3, 0)
         pick(0, 32, lambda n: w.sums_f[n], w.fwd1)
         net.now += 0.5
         parts = []
         rs_plane(net, w.fwd1, w.a1, w.m1, w.b1, w.s, parts)
         yield lambda: len(parts) == 4
-        pre = dot3(w.s[...], win_ref[...])
+        for weight in weights:
+            weight.wait()
+        pre = dot3(w.s[...], w.win[...])
         hidden = pre * (1.0 / (1.0 + jnp.exp(-pre)))
         w.p[...] = pre
         w.h[...] = hidden
         for f in range(2):
             s2 = (w.s2_0, w.s2_1)[f]
             mine = s2.at[pl.ds(net.i * 2, 2)]
-            mine[...] = dot3(hidden, wout_ref[:, f * 128 : f * 128 + 128]).reshape(2, 128, 128)
+            mine[...] = dot3(hidden, w.wout[:, f * 128 : f * 128 + 128]).reshape(2, 128, 128)
             net.now += 0.6
             row_gather(f, lambda u, s2=s2: s2.at[net.i * 2 + u], lambda i, u, s2=s2: s2.at[i * 2 + u], mine, mine, f)
             net.pump()
@@ -500,7 +510,7 @@
             s2 = (w.s2_0, w.s2_1)[f]
             for base in range(0, SLOTS, BLOCK):
                 sums(base, 0, w.acat, lambda left, n: narrow(left, *split(s2[n])), lambda n: w.sums_f.at[n])
-                yield Tick(net, 0.6, 1)
+                yield Tick(net, 0.3, 1)
             pick(0, 32, lambda n: w.sums_f[n], w.fwd2.at[f])
             net.now += 0.5
             rs_plane(net, w.fwd2.at[f], w.a2.at[f], w.m2.at[f], w.b2.at[f], out_ref, [],
@@ -511,7 +521,7 @@
         own_c.wait()
         for base in range(0, SLOTS, BLOCK):
             sums(base, 3, w.atc, wide_product(w.cots), lambda n: w.sums_a.at[n])
-            yield Tick(net, 0.9, 2)
+            yield Tick(net, 0.45, 2)
         pick(3, 16, lambda n: w.sums_a[n], w.adj)
         net.now += 0.5
         parts = []
@@ -538,7 +548,7 @@
         d = w.d[...]
         pre = w.p[...]
         sg = 1.0 / (1.0 + jnp.exp(-pre))
-        d_pre = dot3(d, wout_ref[...], (((1,), (1,)), ((), ()))) * sg * (1.0 + pre * (1.0 - sg))
+        d_pre = dot3(d, w.wout[...], (((1,), (1,)), ((), ()))) * sg * (1.0 + pre * (1.0 - sg))
         grad_in = dot3(jnp.transpose(w.s[...]), d_pre)
         grad_out = dot3(jnp.transpose(w.h[...]), d)
         for c in range(2):
@@ -604,13 +614,13 @@
     outs = pl.pallas_call(
         step_kernel,
         out_shape=outs_shape,
-        in_specs=[SM, SM, ANY, ANY, ANY, VM, VM],
+        in_specs=[SM, SM, ANY, ANY, ANY, ANY, ANY],
         out_specs=(VM, VM, VM),
         scratch_shapes=[pltpu.VMEM(dims, kind) for dims, kind in SCRATCH.values()]
         + [
             pltpu.SemaphoreType.DMA((len(SIZES),)),
             pltpu.SemaphoreType.DMA((COPIES,)),
-            pltpu.SemaphoreType.DMA((SLOTS // CHUNK + 2,)),
+            pltpu.SemaphoreType.DMA((SLOTS // CHUNK + 4,)),
         ],
         compiler_params=pltpu.CompilerParams(
             collective_id=0, has_side_effects=True, vmem_limit_bytes=VMEM_LIMIT),

time: 99.8 us -> 98.9 us (level)
  no operation moved by 1% of the time
where the time goes in v6:
time: 98.9 us; the launch traced here: 98.8 us
  Pallas kernels  98.1 us (99%)
    pallas_call x1, Pallas kernels, per_device(): pl.pallas_call(step_kernel, out_shape=outs_shape, in_specs=[SM, SM, ANY,...  94.5 us

profile of v6, /device:TPU:0, one launch (start us, length us, event | category | flops | bytes accessed | tf_op | source)
XLA Modules:
  0.0 98.8 jit_solution(3561716890116408616)
XLA Ops:
  0.6 1.6 %tables.1 = (s32[8,128]{1,0:T(8,128)}, f32[8,128]{1,0:T(8,128)}) custom-call(s32[1,80]{1,0:T(1,128)} %bitcast.8, s32[1,80]{1,0:T(1,128)} %bitcast.9), custom_call_target="tpu_custom_call" | custom-call | tf_op jit(solution)/shard_map/tables/pallas_call | solution.py:605
  2.3 94.5 %step.1 = (f32[256,256]{1,0:T(8,128)}, f32[128,256]{1,0:T(8,128)}, f32[256,256]{1,0:T(8,128)}) custom-call(s32[8,128]{1,0:T(8,128)} %get-tuple-element.8.int_ref, f32[8,128]{1,0:T(8,128)} %get-tuple-element.9.float_ref, f32[16,2048]{1,0:T(8,128)} %bitcast.7, f32[2,128,256]{2,1,0:T(8,128)} %bitcast.6, f32[80,128,128]{2,1,0:T(8,128)} %bitcast.5, ...), custom_call_target="tpu_custom_call" | custom-call | tf_op jit(solution)/shard_map/step/pallas_call | solution.py:614
  96.8 1.9 %finish.1 = (f32[256,256]{1,0:T(8,128)}, f32[128,256]{1,0:T(8,128)}, f32[256,256]{1,0:T(8,128)}) custom-call(f32[256,256]{1,0:T(8,128)} %get-tuple-element.10.a_ref, f32[128,256]{1,0:T(8,128)} %get-tuple-element.11.b_ref, f32[256,256]{1,0:T(8,128)} %get-tuple-element.12.c_ref), custom_call_target="tpu_custom_call" | custom-call | tf_op jit(solution)/shard_map/finish/pallas_call | solution.py:630
